TPU v7x, 512 devices: a whole 4x4x16 slice. The times are simulated.
512 devices in a mesh: dp: 4 (over y), ep: 128 (over z, x, core).
Axes of the slice: x: 4, y: 4, z: 16, core: 2. Of those that a mesh axis runs over, the one named last changes fastest.
Arguments:
- tokens: bfloat16 [4096, 3584], P(('dp', 'ep')), may hold values from -6 to 6
- expert_ids: int32 [4096, 8], P(('dp', 'ep')), may hold values from 0 to 127, as said below
- route_gates: float32 [4096, 8], P(('dp', 'ep')), may hold values from 0.1 to 1
- w_gate: bfloat16 [128, 3584, 1024], P('ep', None, 'dp'), may hold values from -0.09375 to 0.09375
- w_up: bfloat16 [128, 3584, 1024], P('ep', None, 'dp'), may hold values from -0.09375 to 0.09375
Outputs:
- activations: bfloat16 [4096, 8, 1024], P(('dp', 'ep'))
Inputs may be any that keep to these rules, and one draw needn't show every extreme that they name: `expert_ids`: each row names 8 different experts. Exactly 1 expert, the hot ones, are named by 8 tokens of every device each, and every token names exactly one of them. Any other expert is named by at most 2 tokens of one device, and some such expert is named by exactly 2 tokens of every device.
All inputs are finite; a program needn't handle non-finite values.
Results may differ from a plain program's by a relative error of at most 0.0049.
Values may be sent and summed in bfloat16 or wider, within the bound.
No kernel may reach another device: no remote copies, remote signals or barrier semaphores. Data moves between devices by JAX's collectives and lax.ppermute only.
A program may use at most 128 MiB of HBM per device.

v0:
```python
import functools

import jax
import jax.numpy as jnp
from jax import lax
from jax.experimental import pallas as pl
from jax.experimental.pallas import tpu as pltpu
from jax.sharding import Mesh, PartitionSpec as P


EP_AXES = ("z", "x", "core")
ALL_AXES = ("dp",) + EP_AXES
SLOTS = 2
LANES = 128
CORES = 2
RING = 4
F32 = jnp.float32
BF16 = jnp.bfloat16


def expert_kernel(
    scalar_ref, *refs, part_count, places, tok_rows, aliased
):
    parts, refs = refs[:part_count], refs[part_count:]
    gate0, up0, gate1, up1, *refs = refs
    out_ref, hidden_ref, ids_ref, pay_ref, sems = refs[1:] if aliased else refs
    width, quarter = gate0.shape
    block = sum(part.shape[0] for part in parts)
    homes = block // tok_rows
    rows = jnp.concatenate([part[:, :width] for part in parts], axis=0)
    at = 0
    for part in parts:
        ids_ref[at : at + part.shape[0], :] = part[:, width:].astype(F32)
        at += part.shape[0]
    for place, (gate, up) in enumerate(((gate0, up0), (gate1, up1))):
        gate_part = jnp.dot(rows, gate[...], preferred_element_type=F32)
        up_part = jnp.dot(rows, up[...], preferred_element_type=F32)
        hidden = (gate_part / (1.0 + jnp.exp(-gate_part)) * up_part).astype(BF16)
        for part in range(quarter // LANES):
            hidden_ref[place, part] = hidden[:, part * LANES : (part + 1) * LANES].astype(F32)

    def rows_at(place, tok):
        every = pl.ds(tok, homes, stride=tok_rows)
        parts = [hidden_ref[place, part, every, :] for part in range(quarter // LANES)]
        return jnp.concatenate(parts, axis=1)

    for place in range(CORES):
        expert = scalar_ref[RING * RING + place].astype(F32)
        count = jnp.zeros((homes, 1), F32)
        totals = [jnp.zeros((homes, quarter), F32) for _ in range(SLOTS)]
        for tok in range(tok_rows):
            every = pl.ds(tok, homes, stride=tok_rows)
            value = rows_at(place, tok)
            named = jnp.max(
                jnp.where(ids_ref[every, :] == expert, 1.0, 0.0), axis=1, keepdims=True
            )
            for slot in range(SLOTS):
                take = jnp.where(count == float(slot), named, 0.0)
                totals[slot] = totals[slot] + take * value
            count = count + named
        for slot in range(SLOTS):
            at = (place * SLOTS + slot) * quarter
            pay_ref[:, at : at + quarter] = totals[slot].astype(BF16)
    for tok in range(tok_rows):
        value = jnp.where(scalar_ref[RING * RING + CORES] > 0, rows_at(0, tok), 0.0)
        value += jnp.where(scalar_ref[RING * RING + CORES + 1] > 0, rows_at(1, tok), 0.0)
        at = (CORES * SLOTS + tok) * quarter
        pay_ref[:, at : at + quarter] = value.astype(BF16)

    depth = out_ref.shape[1]
    copies = [
        pltpu.make_async_copy(
            pay_ref.at[pl.ds(line * depth, depth)],
            out_ref.at[scalar_ref[place]],
            sems.at[line],
        )
        for line, place in enumerate(places)
    ]
    for copy in copies:
        copy.start()
    for copy in copies:
        copy.wait()


def serve(scalars, places, piece, weights, so_far, tok_rows, depth):
    quarter = weights[0].shape[1]
    block = sum(part.shape[0] for part in piece)
    lanes = (CORES * SLOTS + tok_rows) * quarter
    operands = [*piece, *weights]
    in_specs = [pl.BlockSpec(memory_space=pltpu.SMEM)]
    in_specs += [pl.BlockSpec(memory_space=pltpu.VMEM) for _ in operands]
    aliases = {}
    if so_far is not None:
        aliases = {1 + len(operands): 0}
        operands.append(so_far)
        in_specs.append(pl.BlockSpec(memory_space=pl.ANY))
    return pl.pallas_call(
        functools.partial(
            expert_kernel,
            part_count=len(piece),
            places=places,
            tok_rows=tok_rows,
            aliased=so_far is not None,
        ),
        in_specs=in_specs,
        out_specs=pl.BlockSpec(memory_space=pl.ANY),
        scratch_shapes=[
            pltpu.VMEM((CORES, quarter // LANES, block, LANES), F32),
            pltpu.VMEM((block, LANES), F32),
            pltpu.VMEM((block // tok_rows, lanes), BF16),
            pltpu.SemaphoreType.DMA((len(places),)),
        ],
        out_shape=jax.ShapeDtypeStruct((RING * RING, depth, lanes), BF16),
        input_output_aliases=aliases,
        compiler_params=pltpu.CompilerParams(vmem_limit_bytes=16 * 2**20),
        cost_estimate=pl.CostEstimate(
            flops=2 * block * weights[0].shape[0] * quarter * 4,
            bytes_accessed=2 * (block * piece[0].shape[1] + 4 * weights[0].size + len(places) * depth * lanes),
            transcendentals=2 * block * quarter,
        ),
        name="expert",
    )(scalars, *operands)


def assemble_kernel(hot_x_ref, near_ref, out_ref, wide_ref, *, tok_rows):
    _, homes, _ = near_ref.shape
    count = out_ref.shape[0] // homes
    quarter = out_ref.shape[1]
    parts = quarter // LANES
    for row in range(count):
        if row < count - tok_rows:
            source, entry = divmod(row, CORES * SLOTS)
        else:
            source, entry = hot_x_ref[0], row - (count - tok_rows) + CORES * SLOTS
        for part in range(parts):
            at = entry * quarter + part * LANES
            wide_ref[part, pl.ds(row, homes, stride=count), :] = near_ref[
                source, :, at : at + LANES
            ].astype(F32)
    for part in range(parts):
        out_ref[:, part * LANES : (part + 1) * LANES] = wide_ref[part].astype(BF16)


def home_kernel(place_ref, gate_ref, rows_ref, out_ref):
    pairs = out_ref.shape[0]
    groups, count, quarter = rows_ref.shape
    row_at = lax.broadcasted_iota(jnp.int32, (pairs, count), 1)
    pick = jnp.where(place_ref[...] == row_at, 1.0, 0.0).astype(BF16)
    gates = gate_ref[...]
    for group in range(groups):
        value = jnp.dot(pick, rows_ref[group], preferred_element_type=F32)
        out_ref[:, group * quarter : (group + 1) * quarter] = (gates * value).astype(BF16)


def per_device(tokens, expert_ids, route_gates, w_gate, w_up, *, sizes):
    tok_rows, top_count = expert_ids.shape
    model_width = tokens.shape[1]
    quarter = w_gate.shape[2]
    groups, depth, width, cores = sizes
    columns = width * cores
    at_y, at_z, at_x, at_core = (lax.axis_index(a).astype(jnp.int32) for a in ALL_AXES)
    own = (at_z * width + at_x) * cores + at_core
    partner = own + 1 - 2 * at_core

    def linear(y, z, x, core):
        return ((y % groups * depth + z) * width + x % width) * cores + core

    def shift(value, first, by):
        pairs = []
        for y in range(groups):
            for z in range(depth):
                for x in range(width):
                    for core in range(cores):
                        along_y = (core == 0) == first
                        to = (y + by, z, x, core) if along_y else (y, z, x + by, core)
                        pairs.append((linear(y, z, x, core), linear(*to)))
        return lax.ppermute(value, ALL_AXES, pairs)

    id_part = jnp.pad(
        expert_ids.astype(BF16), ((0, 0), (0, LANES - top_count)), constant_values=-1
    )
    line = lax.all_gather(
        jnp.concatenate([tokens, id_part], axis=1), "z", axis=0, tiled=True
    )
    expert_ids, w_gate, w_up, line = lax.optimization_barrier((expert_ids, w_gate, w_up, line))

    before = shift(line, True, 1)
    after = shift(line, True, -1)
    line_before = shift(line, False, 1)
    line_after = shift(line, False, -1)
    mine = (w_gate.reshape(model_width, quarter), w_up.reshape(model_width, quarter))
    swap = [(0, 1), (1, 0)]
    theirs = (lax.ppermute(mine[0], "core", swap),)
    theirs = theirs + (lax.ppermute(mine[1], "core", swap),)
    weights = mine + theirs
    mid = jnp.concatenate([before, after], axis=0)
    mid_before = shift(mid, False, 1)
    mid_after = shift(mid, False, -1)
    half = line.shape[0] // 2
    tail = [shift(before[:half], True, 1), shift(after[half:], True, -1)]
    line_far = shift(line_before, False, 1)
    tail = jnp.concatenate(tail, axis=0)
    tail_before = shift(tail, False, 1)
    tail_after = shift(tail, False, -1)
    mid_far = shift(mid_after, False, -1)
    tail_far = shift(tail_before, False, 1)

    named_by = jnp.any(
        expert_ids[:, :, None, None] == expert_ids[None, None, :, :], axis=3
    ).astype(jnp.int32)
    is_hot = jnp.sum(named_by, axis=2) > SLOTS
    tok_at = jnp.arange(tok_rows, dtype=jnp.int32)
    is_before = (tok_at[None, None, :] < tok_at[:, None, None]).astype(jnp.int32)
    slots = jnp.sum(named_by * is_before, axis=2)
    hot_id = jnp.max(jnp.where(is_hot, expert_ids, -1))
    cold_rows = columns * SLOTS
    rows = cold_rows + tok_rows
    place = expert_ids % columns // cores * (cores * SLOTS)
    place = place + jnp.bitwise_xor(expert_ids % cores, at_core) * SLOTS + slots
    place = jnp.where(is_hot, cold_rows + tok_at[:, None], place)
    place = (place + expert_ids // columns * rows).reshape(tok_rows * top_count, 1)

    lane_at = jnp.arange(2 * RING * RING, dtype=jnp.int32)
    offset_of = lambda at: jnp.where(at == 3, 2, jnp.where(at == 2, 1, -at))
    first = offset_of(lane_at % RING)
    second = offset_of(lane_at // RING % RING)
    y_to = (at_y + jnp.where(at_core == 0, first, second)) % groups
    x_to = (at_x + jnp.where(at_core == 0, second, first)) % width
    served_id = jnp.where(lane_at % CORES == 0, own, partner)
    flag = jnp.where(lane_at % RING < CORES, served_id, (served_id == hot_id).astype(jnp.int32))
    scalars = jnp.where(lane_at < RING * RING, x_to * groups + y_to, flag)

    served = None
    calls = (
        (("line", 0), ("mid", 0)),
        (("tail", 0), ("line", 1), ("mid", 1)),
        (("tail", 1), ("line", 2), ("mid", 2)),
        (("tail", 2), ("line", 3)),
        (("tail", 3), ("mid", 3)),
    )
    lines_of = {"line": (0,), "mid": (1, 2), "tail": (3,)}
    parts = {
        "line": (line, line_before, line_after, line_far),
        "mid": (mid, mid_before, mid_after, mid_far),
        "tail": (tail, tail_before, tail_after, tail_far),
    }
    for call in calls:
        places = tuple(RING * piece + j for kind, piece in call for j in lines_of[kind])
        piece_rows = tuple(parts[kind][piece] for kind, piece in call)
        served = serve(scalars, places, piece_rows, weights, served, tok_rows, depth)

    lanes = served.shape[2]
    homes = groups * depth
    near = lax.all_to_all(
        served.reshape(width, homes, lanes), "x", split_axis=0, concat_axis=0, tiled=True
    )
    send = pl.pallas_call(
        functools.partial(assemble_kernel, tok_rows=tok_rows),
        in_specs=[
            pl.BlockSpec(memory_space=pltpu.SMEM),
            pl.BlockSpec(memory_space=pltpu.VMEM),
        ],
        out_shape=jax.ShapeDtypeStruct((homes * rows, quarter), BF16),
        scratch_shapes=[pltpu.VMEM((quarter // LANES, homes * rows, LANES), F32)],
        compiler_params=pltpu.CompilerParams(vmem_limit_bytes=16 * 2**20),
        name="assemble",
    )((hot_id % columns // cores).reshape(1), near).reshape(homes, rows, quarter)
    back = lax.all_to_all(send, ("dp", "z"), split_axis=0, concat_axis=0, tiled=True)
    pairs = tok_rows * top_count
    out = pl.pallas_call(
        home_kernel,
        out_shape=jax.ShapeDtypeStruct((pairs, groups * quarter), BF16),
        compiler_params=pltpu.CompilerParams(vmem_limit_bytes=16 * 2**20),
        name="home",
    )(place, route_gates.reshape(pairs, 1), back.reshape(groups, depth * rows, quarter))
    return out.reshape(tok_rows, top_count, groups * quarter)


def solution(mesh):
    groups = mesh.shape["dp"]
    sizes = (groups, mesh.shape["ep"] // (RING * CORES), RING, CORES)
    fine = Mesh(mesh.devices.reshape(sizes), ALL_AXES)

    def body(*args):
        return per_device(*args, sizes=sizes)

    return jax.shard_map(
        body,
        mesh=fine,
        in_specs=(
            P(ALL_AXES, None),
            P(ALL_AXES, None),
            P(ALL_AXES, None),
            P(EP_AXES, None, "dp"),
            P(EP_AXES, None, "dp"),
        ),
        out_specs=P(ALL_AXES, None, None),
        check_vma=False,
    )
```

profile of v0, /device:TPU:1, one launch (start us, length us, event | category | flops | bytes accessed | tf_op | source)
XLA Modules:
  0.0 243.5 jit_solution(15124968553803567323)
XLA Ops:
  1.5 34.8 %all_gather.3.refs_0_ = bf16[128,3712]{1,0:T(8,128)(2,1)S(1)} all-gather(bf16[8,3712]{1,0:T(8,128)(2,1)S(1)} %fusion.1), channel_id=1, replica_groups=mesh['dp'=4,'z'=16,'x'=4,'core'=2] {'z'}, dimensions={0}, use_global_device_ids=true | all-gather | bytes 1009664 | tf_op jit(solution)/shard_map/all_gather | solution.py:182
  36.3 3.1 %collective-permute-start = (bf16[128,3712]{1,0:T(8,128)(2,1)S(1)}, bf16[128,3712]{1,0:T(8,128)(2,1)S(1)}, u32[]{:S(2)}, u32[]{:S(2)}) collective-permute-start(bf16[128,3712]{1,0:T(8,128)(2,1)S(1)} %all_gather.3.refs_0_), channel_id=1, source_target_pairs={{0,128},{1,3},{2,130},{3,5},{4,132},{5,7},{6,134},{7,1},{8,136},{9... | collective-permute-start | bytes 2850824 | tf_op jit(solution)/shard_map/ppermute | solution.py:177
  39.4 3.4 %collective-permute-start.2 = (bf16[128,3712]{1,0:T(8,128)(2,1)S(1)}, bf16[128,3712]{1,0:T(8,128)(2,1)S(1)}, u32[]{:S(2)}, u32[]{:S(2)}) collective-permute-start(bf16[128,3712]{1,0:T(8,128)(2,1)S(1)} %all_gather.3.refs_0_), channel_id=1, source_target_pairs={{0,384},{1,7},{2,386},{3,1},{4,388},{5,3},{6,390},{7,5},{8,392},{9... | collective-permute-start | bytes 2850824 | tf_op jit(solution)/shard_map/ppermute | solution.py:177
  42.8 9.5 %collective-permute-done = bf16[128,3712]{1,0:T(8,128)(2,1)S(1)} collective-permute-done((bf16[128,3712]{1,0:T(8,128)(2,1)S(1)}, bf16[128,3712]{1,0:T(8,128)(2,1)S(1)}, u32[]{:S(2)}, u32[]{:S(2)}) %collective-permute-start) | collective-permute-done | bytes 950304 | tf_op jit(solution)/shard_map/ppermute | solution.py:177
  55.2 4.8 %collective-permute-start.6 = (bf16[256,3712]{1,0:T(8,128)(2,1)}, bf16[256,3712]{1,0:T(8,128)(2,1)}, u32[]{:S(2)}, u32[]{:S(2)}) collective-permute-start(bf16[256,3712]{1,0:T(8,128)(2,1)} %constant_dynamic-update-slice_fusion.2.refs_1_), channel_id=1, source_target_pairs={{0,6},{1,385},{2,0},{3,387},{4,2},{5,389},{6,4},{7,391},{8,14},{9,... | collective-permute-start | bytes 5701640 | tf_op jit(solution)/shard_map/ppermute | solution.py:177
  60.0 3.1 %collective-permute-start.1 = (bf16[64,3712]{1,0:T(8,128)(2,1)S(1)}, bf16[64,3712]{1,0:T(8,128)(2,1)S(1)}, u32[]{:S(2)}, u32[]{:S(2)}) collective-permute-start(bf16[64,3712]{1,0:T(8,128)(2,1)S(1)} %slice.8), channel_id=1, source_target_pairs={{0,128},{1,3},{2,130},{3,5},{4,132},{5,7},{6,134},{7,1},{8,136},{9... | collective-permute-start | bytes 1425416 | tf_op jit(solution)/shard_map/ppermute | solution.py:177
  63.2 3.4 %collective-permute-start.3 = (bf16[64,3712]{1,0:T(8,128)(2,1)S(1)}, bf16[64,3712]{1,0:T(8,128)(2,1)S(1)}, u32[]{:S(2)}, u32[]{:S(2)}) collective-permute-start(bf16[64,3712]{1,0:T(8,128)(2,1)S(1)} %slice.9), channel_id=1, source_target_pairs={{0,384},{1,7},{2,386},{3,1},{4,388},{5,3},{6,390},{7,5},{8,392},{9... | collective-permute-start | bytes 1425416 | tf_op jit(solution)/shard_map/ppermute | solution.py:177
  66.6 13.6 %collective-permute-start.8 = (bf16[3584,256]{1,0:T(8,128)(2,1)S(1)}, bf16[3584,256]{1,0:T(8,128)(2,1)}, u32[]{:S(2)}, u32[]{:S(2)}) collective-permute-start(bf16[3584,256]{1,0:T(8,128)(2,1)S(1)} %bitcast.7), channel_id=1, source_target_pairs={{0,1},{1,0},{2,3},{3,2},{4,5},{5,4},{6,7},{7,6},{8,9},{9,8},{10,11... | collective-permute-start | bytes 5505032 | tf_op jit(solution)/shard_map/ppermute | solution.py:193
  82.5 2.6 %collective-permute-start.14 = (bf16[256,3712]{1,0:T(8,128)(2,1)}, bf16[256,3712]{1,0:T(8,128)(2,1)}, u32[]{:S(2)}, u32[]{:S(2)}) collective-permute-start(bf16[256,3712]{1,0:T(8,128)(2,1)} %constant_dynamic-update-slice_fusion.2.refs_1_), channel_id=1, source_target_pairs={{0,2},{1,129},{2,4},{3,131},{4,6},{5,133},{6,0},{7,135},{8,10},{9,... | collective-permute-start | bytes 5701640 | tf_op jit(solution)/shard_map/ppermute | solution.py:177
  85.1 5.2 %collective-permute-start.9 = (bf16[3584,256]{1,0:T(8,128)(2,1)}, bf16[3584,256]{1,0:T(8,128)(2,1)}, u32[]{:S(2)}, u32[]{:S(2)}) collective-permute-start(bf16[3584,256]{1,0:T(8,128)(2,1)} %bitcast.2.refs_3_.refs_4_), channel_id=1, source_target_pairs={{0,1},{1,0},{2,3},{3,2},{4,5},{5,4},{6,7},{7,6},{8,9},{9,8},{10,11... | collective-permute-start | bytes 5505032 | tf_op jit(solution)/shard_map/ppermute | solution.py:194
  92.0 4.1 %collective-permute-done.11.refs_1_ = bf16[128,3712]{1,0:T(8,128)(2,1)S(1)} collective-permute-done((bf16[128,3712]{1,0:T(8,128)(2,1)S(1)}, bf16[128,3712]{1,0:T(8,128)(2,1)S(1)}, u32[]{:S(2)}, u32[]{:S(2)}) %collective-permute-start.11) | collective-permute-done | bytes 950304 | tf_op jit(solution)/shard_map/ppermute | solution.py:177
  99.0 4.6 %collective-permute-start.7 = (bf16[256,3712]{1,0:T(8,128)(2,1)}, bf16[256,3712]{1,0:T(8,128)(2,1)}, u32[]{:S(2)}, u32[]{:S(2)}) collective-permute-start(bf16[256,3712]{1,0:T(8,128)(2,1)} %collective-permute-done.6.refs_2_), channel_id=1, source_target_pairs={{0,6},{1,385},{2,0},{3,387},{4,2},{5,389},{6,4},{7,391},{8,14},{9,... | collective-permute-start | bytes 5701640 | tf_op jit(solution)/shard_map/ppermute | solution.py:177
  108.5 3.5 %collective-permute-start.12 = (bf16[128,3712]{1,0:T(8,128)(2,1)}, bf16[128,3712]{1,0:T(8,128)(2,1)S(1)}, u32[]{:S(2)}, u32[]{:S(2)}) collective-permute-start(bf16[128,3712]{1,0:T(8,128)(2,1)} %copy-done.1), channel_id=1, source_target_pairs={{0,2},{1,129},{2,4},{3,131},{4,6},{5,133},{6,0},{7,135},{8,10},{9,... | collective-permute-start | bytes 2850824 | tf_op jit(solution)/shard_map/ppermute | solution.py:177
  112.0 14.8 %collective-permute-done.4.refs_0_ = bf16[128,3712]{1,0:T(8,128)(2,1)} collective-permute-done((bf16[128,3712]{1,0:T(8,128)(2,1)}, bf16[128,3712]{1,0:T(8,128)(2,1)}, u32[]{:S(2)}, u32[]{:S(2)}) %collective-permute-start.4) | collective-permute-done | bytes 950304 | tf_op jit(solution)/shard_map/ppermute | solution.py:177
  128.7 3.5 %collective-permute-start.5 = (bf16[128,3712]{1,0:T(8,128)(2,1)}, bf16[128,3712]{1,0:T(8,128)(2,1)S(1)}, u32[]{:S(2)}, u32[]{:S(2)}) collective-permute-start(bf16[128,3712]{1,0:T(8,128)(2,1)} %collective-permute-done.4.refs_0_), channel_id=1, source_target_pairs={{0,2},{1,129},{2,4},{3,131},{4,6},{5,133},{6,0},{7,135},{8,10},{9,... | collective-permute-start | bytes 2850824 | tf_op jit(solution)/shard_map/ppermute | solution.py:177
  132.3 7.2 %expert.5.refs_7_ = bf16[16,16,3072]{2,1,0:T(8,128)(2,1)} custom-call(s32[32]{0:T(128)S(1)} %compare_select_fusion.12.scalar_ref, bf16[128,3712]{1,0:T(8,128)(2,1)S(1)} %all_gather.3.refs_0_, bf16[256,3712]{1,0:T(8,128)(2,1)} %constant_dynamic-update-slice_fusion.2.refs_1_, bf16[3584,256]{1,0:T(8,128)(2,1)S(1)} %bitcast.8, ...), custom_call_target="tpu_custom_call" | custom-call | flops 2818572288 | bytes 10485760 | tf_op jit(solution)/shard_map/expert/pallas_call | solution.py:97
  139.5 8.6 %expert.6.refs_7_ = bf16[16,16,3072]{2,1,0:T(8,128)(2,1)} custom-call(s32[32]{0:T(128)S(1)} %compare_select_fusion.12.scalar_ref, bf16[128,3712]{1,0:T(8,128)(2,1)} %constant_dynamic-update-slice_fusion.refs_0_, bf16[128,3712]{1,0:T(8,128)(2,1)S(1)} %copy-done.2, bf16[256,3712]{1,0:T(8,128)(2,1)} %collective-permute-done.14.refs_2_, ...), custom_call_target="tpu_custom_call", output_to_operand_aliasing={{}: (8, {})} | custom-call | flops 3758096384 | bytes 11534336 | tf_op jit(solution)/shard_map/expert/pallas_call | solution.py:97
  148.2 8.6 %expert.7.refs_6_ = bf16[16,16,3072]{2,1,0:T(8,128)(2,1)} custom-call(s32[32]{0:T(128)S(1)} %compare_select_fusion.12.scalar_ref, bf16[128,3712]{1,0:T(8,128)(2,1)} %collective-permute-done.4.refs_0_, bf16[128,3712]{1,0:T(8,128)(2,1)S(1)} %collective-permute-done.13.refs_1_, ...), custom_call_target="tpu_custom_call", output_to_operand_aliasing={{}: (8, {})} | custom-call | flops 3758096384 | bytes 11534336 | tf_op jit(solution)/shard_map/expert/pallas_call | solution.py:97
  156.8 5.6 %expert.8.refs_6_ = bf16[16,16,3072]{2,1,0:T(8,128)(2,1)} custom-call(s32[32]{0:T(128)S(1)} %compare_select_fusion.12.scalar_ref, bf16[128,3712]{1,0:T(8,128)(2,1)S(1)} %collective-permute-done.10.refs_0_, bf16[128,3712]{1,0:T(8,128)(2,1)S(1)} %collective-permute-done.12.refs_1_, bf16[3584,256]{1,0:T(8,128)(2,1)S(1)} %bitcast.11, ...), custom_call_target="tpu_custom_call", output_to_operand_aliasing={{}: (7, {})} | custom-call | flops 1879048192 | bytes 9437184 | tf_op jit(solution)/shard_map/expert/pallas_call | solution.py:97
  162.4 7.2 %expert.9 = bf16[16,16,3072]{2,1,0:T(8,128)(2,1)} custom-call(s32[32]{0:T(128)S(1)} %compare_select_fusion.12.scalar_ref, bf16[128,3712]{1,0:T(8,128)(2,1)S(1)} %collective-permute-done.5.refs_0_, bf16[256,3712]{1,0:T(8,128)(2,1)} %collective-permute-done.7.refs_1_, bf16[3584,256]{1,0:T(8,128)(2,1)S(1)} %bitcast.12, ...), custom_call_target="tpu_custom_call", output_to_operand_aliasing={{}: (7, {})} | custom-call | flops 2818572288 | bytes 10485760 | tf_op jit(solution)/shard_map/expert/pallas_call | solution.py:97
  169.6 3.6 %all-to-all-start = ((bf16[4,64,3072]{2,1,0:T(8,128)(2,1)}), bf16[4,64,3072]{2,1,0:T(8,128)(2,1)S(1)}, u32[]{:S(2)}, u32[]{:S(2)}) async-start(bf16[4,64,3072]{2,1,0:T(8,128)(2,1)} %bitcast.3), calls=%async_computation | async-start | bytes 3145728 | tf_op jit(solution)/shard_map/all_to_all | solution.py:254
  175.2 17.4 %all-to-all-done.near_ref = bf16[4,64,3072]{2,1,0:T(8,128)(2,1)S(1)} async-done(((bf16[4,64,3072]{2,1,0:T(8,128)(2,1)}), bf16[4,64,3072]{2,1,0:T(8,128)(2,1)S(1)}, u32[]{:S(2)}, u32[]{:S(2)}) %all-to-all-start) | async-done | bytes 1572896 | tf_op jit(solution)/shard_map/all_to_all | solution.py:254
  194.0 9.5 %all-to-all-start.1 = ((bf16[64,24,256]{2,1,0:T(8,128)(2,1)}), bf16[64,24,256]{2,1,0:T(8,128)(2,1)S(1)}, u32[]{:S(2)}, u32[]{:S(2)}) async-start(bf16[64,24,256]{2,1,0:T(8,128)(2,1)} %bitcast.4), calls=%async_computation.1 | async-start | bytes 1572864 | tf_op jit(solution)/shard_map/all_to_all | solution.py:268
  203.8 38.7 %all-to-all-done.1 = bf16[64,24,256]{2,1,0:T(8,128)(2,1)S(1)} async-done(((bf16[64,24,256]{2,1,0:T(8,128)(2,1)}), bf16[64,24,256]{2,1,0:T(8,128)(2,1)S(1)}, u32[]{:S(2)}, u32[]{:S(2)}) %all-to-all-start.1) | async-done | bytes 786464 | tf_op jit(solution)/shard_map/all_to_all | solution.py:268
  (45 shorter events, 20.6 us)
Async XLA Ops:
  36.3 16.0 %collective-permute-start = (bf16[128,3712]{1,0:T(8,128)(2,1)S(1)}, bf16[128,3712]{1,0:T(8,128)(2,1)S(1)}, u32[]{:S(2)}, u32[]{:S(2)}) collective-permute-start(bf16[128,3712]{1,0:T(8,128)(2,1)S(1)} %all_gather.3.refs_0_), channel_id=1, source_target_pairs={{0,128},{1,3},{2,130},{3,5},{4,132},{5,7},{6,134},{7,1},{8,136},{9... | collective-permute-start | bytes 2850824 | tf_op jit(solution)/shard_map/ppermute | solution.py:177
  39.4 14.8 %collective-permute-start.2 = (bf16[128,3712]{1,0:T(8,128)(2,1)S(1)}, bf16[128,3712]{1,0:T(8,128)(2,1)S(1)}, u32[]{:S(2)}, u32[]{:S(2)}) collective-permute-start(bf16[128,3712]{1,0:T(8,128)(2,1)S(1)} %all_gather.3.refs_0_), channel_id=1, source_target_pairs={{0,384},{1,7},{2,386},{3,1},{4,388},{5,3},{6,390},{7,5},{8,392},{9... | collective-permute-start | bytes 2850824 | tf_op jit(solution)/shard_map/ppermute | solution.py:177
  53.3 13.2 %copy-start = (bf16[1,3584,256]{2,1,0:T(8,128)(2,1)S(1)}, bf16[1,3584,256]{2,1,0:T(8,128)(2,1)}, u32[]{:S(2)}) copy-start(bf16[1,3584,256]{2,1,0:T(8,128)(2,1)} %param.8) | copy-start | bytes 5505028
  55.2 48.5 %copy-start.3 = (s32[8,8]{1,0:T(8,128)S(1)}, s32[8,8]{1,0:T(8,128)}, u32[]{:S(2)}) copy-start(s32[8,8]{1,0:T(8,128)} %param.6) | copy-start | bytes 772
  55.2 43.8 %collective-permute-start.6 = (bf16[256,3712]{1,0:T(8,128)(2,1)}, bf16[256,3712]{1,0:T(8,128)(2,1)}, u32[]{:S(2)}, u32[]{:S(2)}) collective-permute-start(bf16[256,3712]{1,0:T(8,128)(2,1)} %constant_dynamic-update-slice_fusion.2.refs_1_), channel_id=1, source_target_pairs={{0,6},{1,385},{2,0},{3,387},{4,2},{5,389},{6,4},{7,391},{8,14},{9,... | collective-permute-start | bytes 5701640 | tf_op jit(solution)/shard_map/ppermute | solution.py:177
  60.0 22.5 %collective-permute-start.1 = (bf16[64,3712]{1,0:T(8,128)(2,1)S(1)}, bf16[64,3712]{1,0:T(8,128)(2,1)S(1)}, u32[]{:S(2)}, u32[]{:S(2)}) collective-permute-start(bf16[64,3712]{1,0:T(8,128)(2,1)S(1)} %slice.8), channel_id=1, source_target_pairs={{0,128},{1,3},{2,130},{3,5},{4,132},{5,7},{6,134},{7,1},{8,136},{9... | collective-permute-start | bytes 1425416 | tf_op jit(solution)/shard_map/ppermute | solution.py:177
  63.2 21.9 %collective-permute-start.3 = (bf16[64,3712]{1,0:T(8,128)(2,1)S(1)}, bf16[64,3712]{1,0:T(8,128)(2,1)S(1)}, u32[]{:S(2)}, u32[]{:S(2)}) collective-permute-start(bf16[64,3712]{1,0:T(8,128)(2,1)S(1)} %slice.9), channel_id=1, source_target_pairs={{0,384},{1,7},{2,386},{3,1},{4,388},{5,3},{6,390},{7,5},{8,392},{9... | collective-permute-start | bytes 1425416 | tf_op jit(solution)/shard_map/ppermute | solution.py:177
  66.6 38.7 %collective-permute-start.8 = (bf16[3584,256]{1,0:T(8,128)(2,1)S(1)}, bf16[3584,256]{1,0:T(8,128)(2,1)}, u32[]{:S(2)}, u32[]{:S(2)}) collective-permute-start(bf16[3584,256]{1,0:T(8,128)(2,1)S(1)} %bitcast.7), channel_id=1, source_target_pairs={{0,1},{1,0},{2,3},{3,2},{4,5},{5,4},{6,7},{7,6},{8,9},{9,8},{10,11... | collective-permute-start | bytes 5505032 | tf_op jit(solution)/shard_map/ppermute | solution.py:193
  80.2 16.0 %collective-permute-start.11 = (bf16[128,3712]{1,0:T(8,128)(2,1)S(1)}, bf16[128,3712]{1,0:T(8,128)(2,1)S(1)}, u32[]{:S(2)}, u32[]{:S(2)}) collective-permute-start(bf16[128,3712]{1,0:T(8,128)(2,1)S(1)} %all_gather.3.refs_0_), channel_id=1, source_target_pairs={{0,2},{1,129},{2,4},{3,131},{4,6},{5,133},{6,0},{7,135},{8,10},{9,... | collective-permute-start | bytes 2850824 | tf_op jit(solution)/shard_map/ppermute | solution.py:177
  82.5 46.3 %collective-permute-start.14 = (bf16[256,3712]{1,0:T(8,128)(2,1)}, bf16[256,3712]{1,0:T(8,128)(2,1)}, u32[]{:S(2)}, u32[]{:S(2)}) collective-permute-start(bf16[256,3712]{1,0:T(8,128)(2,1)} %constant_dynamic-update-slice_fusion.2.refs_1_), channel_id=1, source_target_pairs={{0,2},{1,129},{2,4},{3,131},{4,6},{5,133},{6,0},{7,135},{8,10},{9,... | collective-permute-start | bytes 5701640 | tf_op jit(solution)/shard_map/ppermute | solution.py:177
  85.1 23.4 %collective-permute-start.9 = (bf16[3584,256]{1,0:T(8,128)(2,1)}, bf16[3584,256]{1,0:T(8,128)(2,1)}, u32[]{:S(2)}, u32[]{:S(2)}) collective-permute-start(bf16[3584,256]{1,0:T(8,128)(2,1)} %bitcast.2.refs_3_.refs_4_), channel_id=1, source_target_pairs={{0,1},{1,0},{2,3},{3,2},{4,5},{5,4},{6,7},{7,6},{8,9},{9,8},{10,11... | collective-permute-start | bytes 5505032 | tf_op jit(solution)/shard_map/ppermute | solution.py:194
  96.2 0.9 copy-start.1
  97.1 29.7 %collective-permute-start.4 = (bf16[128,3712]{1,0:T(8,128)(2,1)}, bf16[128,3712]{1,0:T(8,128)(2,1)}, u32[]{:S(2)}, u32[]{:S(2)}) collective-permute-start(bf16[128,3712]{1,0:T(8,128)(2,1)} %constant_dynamic-update-slice_fusion.refs_0_), channel_id=1, source_target_pairs={{0,2},{1,129},{2,4},{3,131},{4,6},{5,133},{6,0},{7,135},{8,10},{9,... | collective-permute-start | bytes 2850824 | tf_op jit(solution)/shard_map/ppermute | solution.py:177
  99.0 63.4 %collective-permute-start.7 = (bf16[256,3712]{1,0:T(8,128)(2,1)}, bf16[256,3712]{1,0:T(8,128)(2,1)}, u32[]{:S(2)}, u32[]{:S(2)}) collective-permute-start(bf16[256,3712]{1,0:T(8,128)(2,1)} %collective-permute-done.6.refs_2_), channel_id=1, source_target_pairs={{0,6},{1,385},{2,0},{3,387},{4,2},{5,389},{6,4},{7,391},{8,14},{9,... | collective-permute-start | bytes 5701640 | tf_op jit(solution)/shard_map/ppermute | solution.py:177
  105.3 42.9 %collective-permute-start.13 = (bf16[128,3712]{1,0:T(8,128)(2,1)S(1)}, bf16[128,3712]{1,0:T(8,128)(2,1)S(1)}, u32[]{:S(2)}, u32[]{:S(2)}) collective-permute-start(bf16[128,3712]{1,0:T(8,128)(2,1)S(1)} %all_gather.3.refs_0_), channel_id=1, source_target_pairs={{0,6},{1,385},{2,0},{3,387},{4,2},{5,389},{6,4},{7,391},{8,14},{9,... | collective-permute-start | bytes 2850824 | tf_op jit(solution)/shard_map/ppermute | solution.py:177
  108.5 31.0 %copy-start.2 = (bf16[128,3712]{1,0:T(8,128)(2,1)S(1)}, bf16[128,3712]{1,0:T(8,128)(2,1)}, u32[]{:S(2)}) copy-start(bf16[128,3712]{1,0:T(8,128)(2,1)} %copy-done.1) | copy-start | bytes 2850820
  108.5 48.3 %collective-permute-start.12 = (bf16[128,3712]{1,0:T(8,128)(2,1)}, bf16[128,3712]{1,0:T(8,128)(2,1)S(1)}, u32[]{:S(2)}, u32[]{:S(2)}) collective-permute-start(bf16[128,3712]{1,0:T(8,128)(2,1)} %copy-done.1), channel_id=1, source_target_pairs={{0,2},{1,129},{2,4},{3,131},{4,6},{5,133},{6,0},{7,135},{8,10},{9,... | collective-permute-start | bytes 2850824 | tf_op jit(solution)/shard_map/ppermute | solution.py:177
  126.8 30.0 %collective-permute-start.10 = (bf16[128,3712]{1,0:T(8,128)(2,1)}, bf16[128,3712]{1,0:T(8,128)(2,1)S(1)}, u32[]{:S(2)}, u32[]{:S(2)}) collective-permute-start(bf16[128,3712]{1,0:T(8,128)(2,1)} %constant_dynamic-update-slice_fusion.refs_0_), channel_id=1, source_target_pairs={{0,6},{1,385},{2,0},{3,387},{4,2},{5,389},{6,4},{7,391},{8,14},{9,... | collective-permute-start | bytes 2850824 | tf_op jit(solution)/shard_map/ppermute | solution.py:177
  128.7 33.7 %collective-permute-start.5 = (bf16[128,3712]{1,0:T(8,128)(2,1)}, bf16[128,3712]{1,0:T(8,128)(2,1)S(1)}, u32[]{:S(2)}, u32[]{:S(2)}) collective-permute-start(bf16[128,3712]{1,0:T(8,128)(2,1)} %collective-permute-done.4.refs_0_), channel_id=1, source_target_pairs={{0,2},{1,129},{2,4},{3,131},{4,6},{5,133},{6,0},{7,135},{8,10},{9,... | collective-permute-start | bytes 2850824 | tf_op jit(solution)/shard_map/ppermute | solution.py:177
  169.6 23.0 %all-to-all-start = ((bf16[4,64,3072]{2,1,0:T(8,128)(2,1)}), bf16[4,64,3072]{2,1,0:T(8,128)(2,1)S(1)}, u32[]{:S(2)}, u32[]{:S(2)}) async-start(bf16[4,64,3072]{2,1,0:T(8,128)(2,1)} %bitcast.3), calls=%async_computation | async-start | bytes 3145728 | tf_op jit(solution)/shard_map/all_to_all | solution.py:254
  192.6 11.1 %copy-start.4 = (f32[8,8]{1,0:T(8,128)S(1)}, f32[8,8]{1,0:T(8,128)}, u32[]{:S(2)}) copy-start(f32[8,8]{1,0:T(8,128)} %param.7) | copy-start | bytes 772
  194.0 48.5 %all-to-all-start.1 = ((bf16[64,24,256]{2,1,0:T(8,128)(2,1)}), bf16[64,24,256]{2,1,0:T(8,128)(2,1)S(1)}, u32[]{:S(2)}, u32[]{:S(2)}) async-start(bf16[64,24,256]{2,1,0:T(8,128)(2,1)} %bitcast.4), calls=%async_computation.1 | async-start | bytes 1572864 | tf_op jit(solution)/shard_map/all_to_all | solution.py:268
where the time goes:
time: 247 us; the launch traced here: 243 us
  waiting for transfers between devices  85.5 us (35%)
  starting transfers between devices  72 us (29%)
  Pallas kernels  39.6 us (16%)
  blocking collectives  34.8 us (14%)
  local copies, waits for them, and re-layouts  4.85 us (2%)
  other arithmetic  4.5 us (2%)
    ppermute x13, starting transfers between devices, shift(): return lax.ppermute(value, ALL_AXES, pairs)  40 us
    all_to_all x1, waiting for transfers between devices, per_device(): lax.all_to_all(send, ('dp', 'z'), split_axis=0, concat_axis=0, tiled=True)  38.7 us
    pallas_call x5, Pallas kernels, serve(): pl.pallas_call(functools.partial(expert_kernel, part_count=len(piece), pl...  37.2 us
    all_gather x1, blocking collectives, per_device(): lax.all_gather(jnp.concatenate([tokens, id_part], axis=1), 'z', axis=0, t...  34.8 us
    ppermute x13, waiting for transfers between devices, shift(): return lax.ppermute(value, ALL_AXES, pairs)  29.3 us
    all_to_all x1, waiting for transfers between devices, per_device(): lax.all_to_all(served.reshape(width, homes, lanes), 'x', split_axis=0, co...  17.4 us
    ppermute x1, starting transfers between devices, per_device(): theirs = (lax.ppermute(mine[0], 'core', swap),)  13.6 us
    all_to_all x1, starting transfers between devices, per_device(): lax.all_to_all(send, ('dp', 'z'), split_axis=0, concat_axis=0, tiled=True)  9.54 us
  transfers between devices with their start and end apart: 17, of which 6 were waited for; matrix products, arithmetic and copies ran while one was open for 2% of the time, Pallas kernels for 12%

commit v1 on v0

--- a/solution.py
+++ b/solution.py
@@ -198,11 +198,13 @@
     mid_after = shift(mid, False, -1)
     half = line.shape[0] // 2
     tail = [shift(before[:half], True, 1), shift(after[half:], True, -1)]
-    line_far = shift(line_before, False, 1)
+    line_far = shift(line_after, False, -1)
     tail = jnp.concatenate(tail, axis=0)
     tail_before = shift(tail, False, 1)
     tail_after = shift(tail, False, -1)
-    mid_far = shift(mid_after, False, -1)
+    count = line.shape[0]
+    low_far = shift(mid_before[:count], False, 1)
+    high_far = shift(mid_after[count:], False, -1)
     tail_far = shift(tail_before, False, 1)
 
     named_by = jnp.any(
@@ -235,13 +237,15 @@
         (("line", 0), ("mid", 0)),
         (("tail", 0), ("line", 1), ("mid", 1)),
         (("tail", 1), ("line", 2), ("mid", 2)),
-        (("tail", 2), ("line", 3)),
-        (("tail", 3), ("mid", 3)),
-    )
-    lines_of = {"line": (0,), "mid": (1, 2), "tail": (3,)}
+        (("tail", 2), ("line", 3), ("low", 3), ("high", 3)),
+        (("tail", 3),),
+    )
+    lines_of = {"line": (0,), "mid": (1, 2), "low": (1,), "high": (2,), "tail": (3,)}
     parts = {
         "line": (line, line_before, line_after, line_far),
-        "mid": (mid, mid_before, mid_after, mid_far),
+        "mid": (mid, mid_before, mid_after),
+        "low": (None, None, None, low_far),
+        "high": (None, None, None, high_far),
         "tail": (tail, tail_before, tail_after, tail_far),
     }
     for call in calls:

time: 247 us -> 246 us (level)
  waiting for transfers between devices: 85.5 us -> 76.8 us
  starting transfers between devices: 72 us -> 78.7 us
    ppermute x13 -> x14, waiting for transfers between devices: 29.3 us -> 18.1 us  [shift(): return lax.ppermute(value, ALL_AXES, pairs)]
    ppermute x13 -> x14, starting transfers between devices: 40 us -> 45.3 us  [shift(): return lax.ppermute(value, ALL_AXES, pairs)]
    ppermute x1, starting transfers between devices: 13.6 us -> 18.2 us  [per_device(): theirs = (lax.ppermute(mine[0], 'core', swap),)]
    ppermute x1, starting transfers between devices: 5.25 us -> 1.92 us  [per_device(): theirs = theirs + (lax.ppermute(mine[1], 'core', swap),)]
    slice x0 -> x2, local copies, waits for them, and re-layouts: none -> 2.51 us  [the longest x1 1.26 us: per_device(): high_far = shift(mid_after[count:], False, -1)]
  transfers between devices with their start and end apart: 17 -> 18, of which waited for: 6 -> 6; matrix products, arithmetic and copies ran while one was open for 2% -> 4% of each run, Pallas kernels for 12% -> 13%
where the time goes in v1:
time: 246 us; the launch traced here: 243 us
  starting transfers between devices  78.7 us (32%)
  waiting for transfers between devices  76.8 us (31%)
  Pallas kernels  39.3 us (16%)
  blocking collectives  34.8 us (14%)
  local copies, waits for them, and re-layouts  6.45 us (3%)
  other arithmetic  4.5 us (2%)
    ppermute x14, starting transfers between devices, shift(): return lax.ppermute(value, ALL_AXES, pairs)  45.3 us
    all_to_all x1, waiting for transfers between devices, per_device(): lax.all_to_all(send, ('dp', 'z'), split_axis=0, concat_axis=0, tiled=True)  40.1 us
    pallas_call x5, Pallas kernels, serve(): pl.pallas_call(functools.partial(expert_kernel, part_count=len(piece), pl...  37 us
    all_gather x1, blocking collectives, per_device(): lax.all_gather(jnp.concatenate([tokens, id_part], axis=1), 'z', axis=0, t...  34.8 us
    all_to_all x1, waiting for transfers between devices, per_device(): lax.all_to_all(served.reshape(width, homes, lanes), 'x', split_axis=0, co...  18.7 us
    ppermute x1, starting transfers between devices, per_device(): theirs = (lax.ppermute(mine[0], 'core', swap),)  18.2 us
    ppermute x14, waiting for transfers between devices, shift(): return lax.ppermute(value, ALL_AXES, pairs)  18.1 us
    all_to_all x1, starting transfers between devices, per_device(): lax.all_to_all(send, ('dp', 'z'), split_axis=0, concat_axis=0, tiled=True)  9.7 us
  transfers between devices with their start and end apart: 18, of which 6 were waited for; matrix products, arithmetic and copies ran while one was open for 4% of the time, Pallas kernels for 13%

profile of v1, /device:TPU:1, one launch (start us, length us, event | category | flops | bytes accessed | tf_op | source)
XLA Modules:
  0.0 242.9 jit_solution(10660151292638733039)
XLA Ops:
  1.5 34.8 %all_gather.3.refs_0_ = bf16[128,3712]{1,0:T(8,128)(2,1)S(1)} all-gather(bf16[8,3712]{1,0:T(8,128)(2,1)S(1)} %fusion.1), channel_id=1, replica_groups=mesh['dp'=4,'z'=16,'x'=4,'core'=2] {'z'}, dimensions={0}, use_global_device_ids=true | all-gather | bytes 1009664 | tf_op jit(solution)/shard_map/all_gather | solution.py:182
  36.3 3.1 %collective-permute-start = (bf16[128,3712]{1,0:T(8,128)(2,1)S(1)}, bf16[128,3712]{1,0:T(8,128)(2,1)S(1)}, u32[]{:S(2)}, u32[]{:S(2)}) collective-permute-start(bf16[128,3712]{1,0:T(8,128)(2,1)S(1)} %all_gather.3.refs_0_), channel_id=1, source_target_pairs={{0,128},{1,3},{2,130},{3,5},{4,132},{5,7},{6,134},{7,1},{8,136},{9... | collective-permute-start | bytes 2850824 | tf_op jit(solution)/shard_map/ppermute | solution.py:177
  39.4 3.4 %collective-permute-start.2 = (bf16[128,3712]{1,0:T(8,128)(2,1)S(1)}, bf16[128,3712]{1,0:T(8,128)(2,1)S(1)}, u32[]{:S(2)}, u32[]{:S(2)}) collective-permute-start(bf16[128,3712]{1,0:T(8,128)(2,1)S(1)} %all_gather.3.refs_0_), channel_id=1, source_target_pairs={{0,384},{1,7},{2,386},{3,1},{4,388},{5,3},{6,390},{7,5},{8,392},{9... | collective-permute-start | bytes 2850824 | tf_op jit(solution)/shard_map/ppermute | solution.py:177
  42.8 4.6 %collective-permute-start.9 = (bf16[128,3712]{1,0:T(8,128)(2,1)S(1)}, bf16[128,3712]{1,0:T(8,128)(2,1)S(1)}, u32[]{:S(2)}, u32[]{:S(2)}) collective-permute-start(bf16[128,3712]{1,0:T(8,128)(2,1)S(1)} %all_gather.3.refs_0_), channel_id=1, source_target_pairs={{0,6},{1,385},{2,0},{3,387},{4,2},{5,389},{6,4},{7,391},{8,14},{9,... | collective-permute-start | bytes 2850824 | tf_op jit(solution)/shard_map/ppermute | solution.py:177
  47.4 4.8 %collective-permute-done = bf16[128,3712]{1,0:T(8,128)(2,1)S(1)} collective-permute-done((bf16[128,3712]{1,0:T(8,128)(2,1)S(1)}, bf16[128,3712]{1,0:T(8,128)(2,1)S(1)}, u32[]{:S(2)}, u32[]{:S(2)}) %collective-permute-start) | collective-permute-done | bytes 950304 | tf_op jit(solution)/shard_map/ppermute | solution.py:177
  55.2 3.3 %collective-permute-start.11 = (bf16[256,3712]{1,0:T(8,128)(2,1)}, bf16[256,3712]{1,0:T(8,128)(2,1)}, u32[]{:S(2)}, u32[]{:S(2)}) collective-permute-start(bf16[256,3712]{1,0:T(8,128)(2,1)} %constant_dynamic-update-slice_fusion.2.refs_1_), channel_id=1, source_target_pairs={{0,2},{1,129},{2,4},{3,131},{4,6},{5,133},{6,0},{7,135},{8,10},{9,... | collective-permute-start | bytes 5701640 | tf_op jit(solution)/shard_map/ppermute | solution.py:177
  58.6 3.1 %collective-permute-start.1 = (bf16[64,3712]{1,0:T(8,128)(2,1)S(1)}, bf16[64,3712]{1,0:T(8,128)(2,1)S(1)}, u32[]{:S(2)}, u32[]{:S(2)}) collective-permute-start(bf16[64,3712]{1,0:T(8,128)(2,1)S(1)} %slice.16), channel_id=1, source_target_pairs={{0,128},{1,3},{2,130},{3,5},{4,132},{5,7},{6,134},{7,1},{8,136},{9... | collective-permute-start | bytes 1425416 | tf_op jit(solution)/shard_map/ppermute | solution.py:177
  61.7 3.4 %collective-permute-start.13 = (bf16[256,3712]{1,0:T(8,128)(2,1)}, bf16[256,3712]{1,0:T(8,128)(2,1)}, u32[]{:S(2)}, u32[]{:S(2)}) collective-permute-start(bf16[256,3712]{1,0:T(8,128)(2,1)} %constant_dynamic-update-slice_fusion.2.refs_1_), channel_id=1, source_target_pairs={{0,6},{1,385},{2,0},{3,387},{4,2},{5,389},{6,4},{7,391},{8,14},{9,... | collective-permute-start | bytes 5701640 | tf_op jit(solution)/shard_map/ppermute | solution.py:177
  65.1 18.2 %collective-permute-start.6 = (bf16[3584,256]{1,0:T(8,128)(2,1)S(1)}, bf16[3584,256]{1,0:T(8,128)(2,1)}, u32[]{:S(2)}, u32[]{:S(2)}) collective-permute-start(bf16[3584,256]{1,0:T(8,128)(2,1)S(1)} %bitcast.7), channel_id=1, source_target_pairs={{0,1},{1,0},{2,3},{3,2},{4,5},{5,4},{6,7},{7,6},{8,9},{9,8},{10,11... | collective-permute-start | bytes 5505032 | tf_op jit(solution)/shard_map/ppermute | solution.py:193
  88.1 12.1 %collective-permute-done.3 = bf16[64,3712]{1,0:T(8,128)(2,1)S(1)} collective-permute-done((bf16[64,3712]{1,0:T(8,128)(2,1)S(1)}, bf16[64,3712]{1,0:T(8,128)(2,1)S(1)}, u32[]{:S(2)}, u32[]{:S(2)}) %collective-permute-start.3) | collective-permute-done | bytes 475168 | tf_op jit(solution)/shard_map/ppermute | solution.py:177
  100.2 3.2 %collective-permute-start.15 = (bf16[128,3712]{1,0:T(8,128)(2,1)S(1)}, bf16[128,3712]{1,0:T(8,128)(2,1)}, u32[]{:S(2)}, u32[]{:S(2)}) collective-permute-start(bf16[128,3712]{1,0:T(8,128)(2,1)S(1)} %all_gather.3.refs_0_), channel_id=1, source_target_pairs={{0,2},{1,129},{2,4},{3,131},{4,6},{5,133},{6,0},{7,135},{8,10},{9,... | collective-permute-start | bytes 2850824 | tf_op jit(solution)/shard_map/ppermute | solution.py:177
  104.2 5.1 %collective-permute-start.4 = (bf16[128,3712]{1,0:T(8,128)(2,1)}, bf16[128,3712]{1,0:T(8,128)(2,1)}, u32[]{:S(2)}, u32[]{:S(2)}) collective-permute-start(bf16[128,3712]{1,0:T(8,128)(2,1)} %constant_dynamic-update-slice_fusion.refs_0_), channel_id=1, source_target_pairs={{0,2},{1,129},{2,4},{3,131},{4,6},{5,133},{6,0},{7,135},{8,10},{9,... | collective-permute-start | bytes 2850824 | tf_op jit(solution)/shard_map/ppermute | solution.py:177
  117.0 3.6 %collective-permute-start.8 = (bf16[128,3712]{1,0:T(8,128)(2,1)}, bf16[128,3712]{1,0:T(8,128)(2,1)S(1)}, u32[]{:S(2)}, u32[]{:S(2)}) collective-permute-start(bf16[128,3712]{1,0:T(8,128)(2,1)} %constant_dynamic-update-slice_fusion.refs_0_), channel_id=1, source_target_pairs={{0,6},{1,385},{2,0},{3,387},{4,2},{5,389},{6,4},{7,391},{8,14},{9,... | collective-permute-start | bytes 2850824 | tf_op jit(solution)/shard_map/ppermute | solution.py:177
  122.6 4.6 %collective-permute-start.14 = (bf16[128,3712]{1,0:T(8,128)(2,1)S(1)}, bf16[128,3712]{1,0:T(8,128)(2,1)S(1)}, u32[]{:S(2)}, u32[]{:S(2)}) collective-permute-start(bf16[128,3712]{1,0:T(8,128)(2,1)S(1)} %slice.19), channel_id=1, source_target_pairs={{0,6},{1,385},{2,0},{3,387},{4,2},{5,389},{6,4},{7,391},{8,14},{9,... | collective-permute-start | bytes 2850824 | tf_op jit(solution)/shard_map/ppermute | solution.py:177
  127.2 7.2 %expert.5.refs_7_ = bf16[16,16,3072]{2,1,0:T(8,128)(2,1)} custom-call(s32[32]{0:T(128)S(1)} %compare_select_fusion.12.scalar_ref, bf16[128,3712]{1,0:T(8,128)(2,1)S(1)} %all_gather.3.refs_0_, bf16[256,3712]{1,0:T(8,128)(2,1)} %constant_dynamic-update-slice_fusion.2.refs_1_, bf16[3584,256]{1,0:T(8,128)(2,1)S(1)} %bitcast.8, ...), custom_call_target="tpu_custom_call" | custom-call | flops 2818572288 | bytes 10485760 | tf_op jit(solution)/shard_map/expert/pallas_call | solution.py:97
  134.4 2.1 collective-permute-start.5
  136.5 8.9 %expert.6.refs_7_ = bf16[16,16,3072]{2,1,0:T(8,128)(2,1)} custom-call(s32[32]{0:T(128)S(1)} %compare_select_fusion.12.scalar_ref, bf16[128,3712]{1,0:T(8,128)(2,1)} %constant_dynamic-update-slice_fusion.refs_0_, bf16[128,3712]{1,0:T(8,128)(2,1)} %collective-permute-done.15.refs_1_, ...), custom_call_target="tpu_custom_call", output_to_operand_aliasing={{}: (8, {})} | custom-call | flops 3758096384 | bytes 11534336 | tf_op jit(solution)/shard_map/expert/pallas_call | solution.py:97
  145.4 8.6 %expert.7.refs_8_ = bf16[16,16,3072]{2,1,0:T(8,128)(2,1)} custom-call(s32[32]{0:T(128)S(1)} %compare_select_fusion.12.scalar_ref, bf16[128,3712]{1,0:T(8,128)(2,1)} %collective-permute-done.4.refs_0_, bf16[128,3712]{1,0:T(8,128)(2,1)S(1)} %copy-done.2, bf16[256,3712]{1,0:T(8,128)(2,1)} %collective-permute-done.13.refs_2_, ...), custom_call_target="tpu_custom_call", output_to_operand_aliasing={{}: (8, {})} | custom-call | flops 3758096384 | bytes 11534336 | tf_op jit(solution)/shard_map/expert/pallas_call | solution.py:97
  154.0 7.8 %expert.8.refs_5_ = bf16[16,16,3072]{2,1,0:T(8,128)(2,1)} custom-call(s32[32]{0:T(128)S(1)} %compare_select_fusion.12.scalar_ref, bf16[128,3712]{1,0:T(8,128)(2,1)S(1)} %collective-permute-done.8.refs_0_, bf16[128,3712]{1,0:T(8,128)(2,1)S(1)} %collective-permute-done.10.refs_1_, ...), custom_call_target="tpu_custom_call", output_to_operand_aliasing={{}: (9, {})} | custom-call | flops 3758096384 | bytes 11534336 | tf_op jit(solution)/shard_map/expert/pallas_call | solution.py:97
  161.8 4.5 %expert.9 = bf16[16,16,3072]{2,1,0:T(8,128)(2,1)} custom-call(s32[32]{0:T(128)S(1)} %compare_select_fusion.12.scalar_ref, bf16[128,3712]{1,0:T(8,128)(2,1)S(1)} %collective-permute-done.5.refs_0_, bf16[3584,256]{1,0:T(8,128)(2,1)S(1)} %bitcast.12, bf16[3584,256]{1,0:T(8,128)(2,1)} %bitcast.2.refs_3_.refs_4_.refs_5_.refs_2_, ...), custom_call_target="tpu_custom_call", output_to_operand_aliasing={{}: (6, {})} | custom-call | flops 939524096 | bytes 8388608 | tf_op jit(solution)/shard_map/expert/pallas_call | solution.py:97
  166.4 3.6 %all-to-all-start = ((bf16[4,64,3072]{2,1,0:T(8,128)(2,1)}), bf16[4,64,3072]{2,1,0:T(8,128)(2,1)S(1)}, u32[]{:S(2)}, u32[]{:S(2)}) async-start(bf16[4,64,3072]{2,1,0:T(8,128)(2,1)} %bitcast.3), calls=%async_computation | async-start | bytes 3145728 | tf_op jit(solution)/shard_map/all_to_all | solution.py:258
  171.9 18.7 %all-to-all-done.near_ref = bf16[4,64,3072]{2,1,0:T(8,128)(2,1)S(1)} async-done(((bf16[4,64,3072]{2,1,0:T(8,128)(2,1)}), bf16[4,64,3072]{2,1,0:T(8,128)(2,1)S(1)}, u32[]{:S(2)}, u32[]{:S(2)}) %all-to-all-start) | async-done | bytes 1572896 | tf_op jit(solution)/shard_map/all_to_all | solution.py:258
  192.0 9.7 %all-to-all-start.1 = ((bf16[64,24,256]{2,1,0:T(8,128)(2,1)}), bf16[64,24,256]{2,1,0:T(8,128)(2,1)S(1)}, u32[]{:S(2)}, u32[]{:S(2)}) async-start(bf16[64,24,256]{2,1,0:T(8,128)(2,1)} %bitcast.4), calls=%async_computation.1 | async-start | bytes 1572864 | tf_op jit(solution)/shard_map/all_to_all | solution.py:272
  201.9 40.1 %all-to-all-done.1 = bf16[64,24,256]{2,1,0:T(8,128)(2,1)S(1)} async-done(((bf16[64,24,256]{2,1,0:T(8,128)(2,1)}), bf16[64,24,256]{2,1,0:T(8,128)(2,1)S(1)}, u32[]{:S(2)}, u32[]{:S(2)}) %all-to-all-start.1) | async-done | bytes 786464 | tf_op jit(solution)/shard_map/all_to_all | solution.py:272
  (49 shorter events, 22.2 us)
Async XLA Ops:
  36.3 16.0 %collective-permute-start = (bf16[128,3712]{1,0:T(8,128)(2,1)S(1)}, bf16[128,3712]{1,0:T(8,128)(2,1)S(1)}, u32[]{:S(2)}, u32[]{:S(2)}) collective-permute-start(bf16[128,3712]{1,0:T(8,128)(2,1)S(1)} %all_gather.3.refs_0_), channel_id=1, source_target_pairs={{0,128},{1,3},{2,130},{3,5},{4,132},{5,7},{6,134},{7,1},{8,136},{9... | collective-permute-start | bytes 2850824 | tf_op jit(solution)/shard_map/ppermute | solution.py:177
  39.4 14.8 %collective-permute-start.2 = (bf16[128,3712]{1,0:T(8,128)(2,1)S(1)}, bf16[128,3712]{1,0:T(8,128)(2,1)S(1)}, u32[]{:S(2)}, u32[]{:S(2)}) collective-permute-start(bf16[128,3712]{1,0:T(8,128)(2,1)S(1)} %all_gather.3.refs_0_), channel_id=1, source_target_pairs={{0,384},{1,7},{2,386},{3,1},{4,388},{5,3},{6,390},{7,5},{8,392},{9... | collective-permute-start | bytes 2850824 | tf_op jit(solution)/shard_map/ppermute | solution.py:177
  42.8 40.5 %collective-permute-start.9 = (bf16[128,3712]{1,0:T(8,128)(2,1)S(1)}, bf16[128,3712]{1,0:T(8,128)(2,1)S(1)}, u32[]{:S(2)}, u32[]{:S(2)}) collective-permute-start(bf16[128,3712]{1,0:T(8,128)(2,1)S(1)} %all_gather.3.refs_0_), channel_id=1, source_target_pairs={{0,6},{1,385},{2,0},{3,387},{4,2},{5,389},{6,4},{7,391},{8,14},{9,... | collective-permute-start | bytes 2850824 | tf_op jit(solution)/shard_map/ppermute | solution.py:177
  53.3 11.8 %copy-start = (bf16[1,3584,256]{2,1,0:T(8,128)(2,1)S(1)}, bf16[1,3584,256]{2,1,0:T(8,128)(2,1)}, u32[]{:S(2)}) copy-start(bf16[1,3584,256]{2,1,0:T(8,128)(2,1)} %param.8) | copy-start | bytes 5505028
  55.2 54.2 %copy-start.3 = (s32[8,8]{1,0:T(8,128)S(1)}, s32[8,8]{1,0:T(8,128)}, u32[]{:S(2)}) copy-start(s32[8,8]{1,0:T(8,128)} %param.6) | copy-start | bytes 772
  55.2 49.0 %collective-permute-start.11 = (bf16[256,3712]{1,0:T(8,128)(2,1)}, bf16[256,3712]{1,0:T(8,128)(2,1)}, u32[]{:S(2)}, u32[]{:S(2)}) collective-permute-start(bf16[256,3712]{1,0:T(8,128)(2,1)} %constant_dynamic-update-slice_fusion.2.refs_1_), channel_id=1, source_target_pairs={{0,2},{1,129},{2,4},{3,131},{4,6},{5,133},{6,0},{7,135},{8,10},{9,... | collective-permute-start | bytes 5701640 | tf_op jit(solution)/shard_map/ppermute | solution.py:177
  58.6 26.7 %collective-permute-start.1 = (bf16[64,3712]{1,0:T(8,128)(2,1)S(1)}, bf16[64,3712]{1,0:T(8,128)(2,1)S(1)}, u32[]{:S(2)}, u32[]{:S(2)}) collective-permute-start(bf16[64,3712]{1,0:T(8,128)(2,1)S(1)} %slice.16), channel_id=1, source_target_pairs={{0,128},{1,3},{2,130},{3,5},{4,132},{5,7},{6,134},{7,1},{8,136},{9... | collective-permute-start | bytes 1425416 | tf_op jit(solution)/shard_map/ppermute | solution.py:177
  61.7 51.9 %collective-permute-start.13 = (bf16[256,3712]{1,0:T(8,128)(2,1)}, bf16[256,3712]{1,0:T(8,128)(2,1)}, u32[]{:S(2)}, u32[]{:S(2)}) collective-permute-start(bf16[256,3712]{1,0:T(8,128)(2,1)} %constant_dynamic-update-slice_fusion.2.refs_1_), channel_id=1, source_target_pairs={{0,6},{1,385},{2,0},{3,387},{4,2},{5,389},{6,4},{7,391},{8,14},{9,... | collective-permute-start | bytes 5701640 | tf_op jit(solution)/shard_map/ppermute | solution.py:177
  65.1 55.6 %collective-permute-start.6 = (bf16[3584,256]{1,0:T(8,128)(2,1)S(1)}, bf16[3584,256]{1,0:T(8,128)(2,1)}, u32[]{:S(2)}, u32[]{:S(2)}) collective-permute-start(bf16[3584,256]{1,0:T(8,128)(2,1)S(1)} %bitcast.7), channel_id=1, source_target_pairs={{0,1},{1,0},{2,3},{3,2},{4,5},{5,4},{6,7},{7,6},{8,9},{9,8},{10,11... | collective-permute-start | bytes 5505032 | tf_op jit(solution)/shard_map/ppermute | solution.py:193
  83.3 4.8 %copy-start.1 = (bf16[128,3712]{1,0:T(8,128)(2,1)}, bf16[128,3712]{1,0:T(8,128)(2,1)S(1)}, u32[]{:S(2)}) copy-start(bf16[128,3712]{1,0:T(8,128)(2,1)S(1)} %collective-permute-done.9.refs_1_) | copy-start | bytes 2850820
  83.3 39.3 %collective-permute-start.7 = (bf16[3584,256]{1,0:T(8,128)(2,1)}, bf16[3584,256]{1,0:T(8,128)(2,1)}, u32[]{:S(2)}, u32[]{:S(2)}) collective-permute-start(bf16[3584,256]{1,0:T(8,128)(2,1)} %bitcast.2.refs_3_.refs_4_.refs_5_.refs_2_), channel_id=1, source_target_pairs={{0,1},{1,0},{2,3},{3,2},{4,5},{5,4},{6,7},{7,6},{8,9},{9,8},{10,11... | collective-permute-start | bytes 5505032 | tf_op jit(solution)/shard_map/ppermute | solution.py:194
  85.3 14.9 %collective-permute-start.3 = (bf16[64,3712]{1,0:T(8,128)(2,1)S(1)}, bf16[64,3712]{1,0:T(8,128)(2,1)S(1)}, u32[]{:S(2)}, u32[]{:S(2)}) collective-permute-start(bf16[64,3712]{1,0:T(8,128)(2,1)S(1)} %slice.17), channel_id=1, source_target_pairs={{0,384},{1,7},{2,386},{3,1},{4,388},{5,3},{6,390},{7,5},{8,392},{9... | collective-permute-start | bytes 1425416 | tf_op jit(solution)/shard_map/ppermute | solution.py:177
  100.2 16.8 %collective-permute-start.15 = (bf16[128,3712]{1,0:T(8,128)(2,1)S(1)}, bf16[128,3712]{1,0:T(8,128)(2,1)}, u32[]{:S(2)}, u32[]{:S(2)}) collective-permute-start(bf16[128,3712]{1,0:T(8,128)(2,1)S(1)} %all_gather.3.refs_0_), channel_id=1, source_target_pairs={{0,2},{1,129},{2,4},{3,131},{4,6},{5,133},{6,0},{7,135},{8,10},{9,... | collective-permute-start | bytes 2850824 | tf_op jit(solution)/shard_map/ppermute | solution.py:177
  104.2 30.1 %collective-permute-start.4 = (bf16[128,3712]{1,0:T(8,128)(2,1)}, bf16[128,3712]{1,0:T(8,128)(2,1)}, u32[]{:S(2)}, u32[]{:S(2)}) collective-permute-start(bf16[128,3712]{1,0:T(8,128)(2,1)} %constant_dynamic-update-slice_fusion.refs_0_), channel_id=1, source_target_pairs={{0,2},{1,129},{2,4},{3,131},{4,6},{5,133},{6,0},{7,135},{8,10},{9,... | collective-permute-start | bytes 2850824 | tf_op jit(solution)/shard_map/ppermute | solution.py:177
  109.4 4.2 %copy-start.2 = (bf16[128,3712]{1,0:T(8,128)(2,1)S(1)}, bf16[128,3712]{1,0:T(8,128)(2,1)}, u32[]{:S(2)}) copy-start(bf16[128,3712]{1,0:T(8,128)(2,1)} %copy-done.1) | copy-start | bytes 2850820
  113.6 40.4 %collective-permute-start.10 = (bf16[128,3712]{1,0:T(8,128)(2,1)S(1)}, bf16[128,3712]{1,0:T(8,128)(2,1)S(1)}, u32[]{:S(2)}, u32[]{:S(2)}) collective-permute-start(bf16[128,3712]{1,0:T(8,128)(2,1)S(1)} %copy-done.2), channel_id=1, source_target_pairs={{0,6},{1,385},{2,0},{3,387},{4,2},{5,389},{6,4},{7,391},{8,14},{9,... | collective-permute-start | bytes 2850824 | tf_op jit(solution)/shard_map/ppermute | solution.py:177
  117.0 37.0 %collective-permute-start.8 = (bf16[128,3712]{1,0:T(8,128)(2,1)}, bf16[128,3712]{1,0:T(8,128)(2,1)S(1)}, u32[]{:S(2)}, u32[]{:S(2)}) collective-permute-start(bf16[128,3712]{1,0:T(8,128)(2,1)} %constant_dynamic-update-slice_fusion.refs_0_), channel_id=1, source_target_pairs={{0,6},{1,385},{2,0},{3,387},{4,2},{5,389},{6,4},{7,391},{8,14},{9,... | collective-permute-start | bytes 2850824 | tf_op jit(solution)/shard_map/ppermute | solution.py:177
  120.7 33.4 %collective-permute-start.12 = (bf16[128,3712]{1,0:T(8,128)(2,1)S(1)}, bf16[128,3712]{1,0:T(8,128)(2,1)S(1)}, u32[]{:S(2)}, u32[]{:S(2)}) collective-permute-start(bf16[128,3712]{1,0:T(8,128)(2,1)S(1)} %slice.18), channel_id=1, source_target_pairs={{0,2},{1,129},{2,4},{3,131},{4,6},{5,133},{6,0},{7,135},{8,10},{9,... | collective-permute-start | bytes 2850824 | tf_op jit(solution)/shard_map/ppermute | solution.py:177
  122.6 31.4 %collective-permute-start.14 = (bf16[128,3712]{1,0:T(8,128)(2,1)S(1)}, bf16[128,3712]{1,0:T(8,128)(2,1)S(1)}, u32[]{:S(2)}, u32[]{:S(2)}) collective-permute-start(bf16[128,3712]{1,0:T(8,128)(2,1)S(1)} %slice.19), channel_id=1, source_target_pairs={{0,6},{1,385},{2,0},{3,387},{4,2},{5,389},{6,4},{7,391},{8,14},{9,... | collective-permute-start | bytes 2850824 | tf_op jit(solution)/shard_map/ppermute | solution.py:177
  134.4 27.4 %collective-permute-start.5 = (bf16[128,3712]{1,0:T(8,128)(2,1)}, bf16[128,3712]{1,0:T(8,128)(2,1)S(1)}, u32[]{:S(2)}, u32[]{:S(2)}) collective-permute-start(bf16[128,3712]{1,0:T(8,128)(2,1)} %collective-permute-done.4.refs_0_), channel_id=1, source_target_pairs={{0,2},{1,129},{2,4},{3,131},{4,6},{5,133},{6,0},{7,135},{8,10},{9,... | collective-permute-start | bytes 2850824 | tf_op jit(solution)/shard_map/ppermute | solution.py:177
  166.4 24.2 %all-to-all-start = ((bf16[4,64,3072]{2,1,0:T(8,128)(2,1)}), bf16[4,64,3072]{2,1,0:T(8,128)(2,1)S(1)}, u32[]{:S(2)}, u32[]{:S(2)}) async-start(bf16[4,64,3072]{2,1,0:T(8,128)(2,1)} %bitcast.3), calls=%async_computation | async-start | bytes 3145728 | tf_op jit(solution)/shard_map/all_to_all | solution.py:258
  190.6 11.3 %copy-start.4 = (f32[8,8]{1,0:T(8,128)S(1)}, f32[8,8]{1,0:T(8,128)}, u32[]{:S(2)}) copy-start(f32[8,8]{1,0:T(8,128)} %param.7) | copy-start | bytes 772
  192.0 50.0 %all-to-all-start.1 = ((bf16[64,24,256]{2,1,0:T(8,128)(2,1)}), bf16[64,24,256]{2,1,0:T(8,128)(2,1)S(1)}, u32[]{:S(2)}, u32[]{:S(2)}) async-start(bf16[64,24,256]{2,1,0:T(8,128)(2,1)} %bitcast.4), calls=%async_computation.1 | async-start | bytes 1572864 | tf_op jit(solution)/shard_map/all_to_all | solution.py:272

commit v2 on v0

--- a/solution.py
+++ b/solution.py
@@ -19,12 +19,12 @@
 
 
 def expert_kernel(
-    scalar_ref, *refs, part_count, places, tok_rows, aliased
+    scalar_ref, line_ref, mid_ref, tail_ref, *rest, number, tok_rows, aliased
 ):
-    parts, refs = refs[:part_count], refs[part_count:]
-    gate0, up0, gate1, up1, *refs = refs
+    gate0, up0, gate1, up1, *refs = rest
     out_ref, hidden_ref, ids_ref, pay_ref, sems = refs[1:] if aliased else refs
     width, quarter = gate0.shape
+    parts = (line_ref, mid_ref, tail_ref)
     block = sum(part.shape[0] for part in parts)
     homes = block // tok_rows
     rows = jnp.concatenate([part[:, :width] for part in parts], axis=0)
@@ -71,10 +71,10 @@
     copies = [
         pltpu.make_async_copy(
             pay_ref.at[pl.ds(line * depth, depth)],
-            out_ref.at[scalar_ref[place]],
+            out_ref.at[scalar_ref[RING * number + line]],
             sems.at[line],
         )
-        for line, place in enumerate(places)
+        for line in range(RING)
     ]
     for copy in copies:
         copy.start()
@@ -82,7 +82,7 @@
         copy.wait()
 
 
-def serve(scalars, places, piece, weights, so_far, tok_rows, depth):
+def serve(scalars, number, piece, weights, so_far, tok_rows, depth):
     quarter = weights[0].shape[1]
     block = sum(part.shape[0] for part in piece)
     lanes = (CORES * SLOTS + tok_rows) * quarter
@@ -96,11 +96,7 @@
         in_specs.append(pl.BlockSpec(memory_space=pl.ANY))
     return pl.pallas_call(
         functools.partial(
-            expert_kernel,
-            part_count=len(piece),
-            places=places,
-            tok_rows=tok_rows,
-            aliased=so_far is not None,
+            expert_kernel, number=number, tok_rows=tok_rows, aliased=so_far is not None
         ),
         in_specs=in_specs,
         out_specs=pl.BlockSpec(memory_space=pl.ANY),
@@ -108,14 +104,14 @@
             pltpu.VMEM((CORES, quarter // LANES, block, LANES), F32),
             pltpu.VMEM((block, LANES), F32),
             pltpu.VMEM((block // tok_rows, lanes), BF16),
-            pltpu.SemaphoreType.DMA((len(places),)),
+            pltpu.SemaphoreType.DMA((RING,)),
         ],
         out_shape=jax.ShapeDtypeStruct((RING * RING, depth, lanes), BF16),
         input_output_aliases=aliases,
         compiler_params=pltpu.CompilerParams(vmem_limit_bytes=16 * 2**20),
         cost_estimate=pl.CostEstimate(
             flops=2 * block * weights[0].shape[0] * quarter * 4,
-            bytes_accessed=2 * (block * piece[0].shape[1] + 4 * weights[0].size + len(places) * depth * lanes),
+            bytes_accessed=2 * (block * piece[0].shape[1] + 4 * weights[0].size + RING * depth * lanes),
             transcendentals=2 * block * quarter,
         ),
         name="expert",
@@ -231,23 +227,14 @@
     scalars = jnp.where(lane_at < RING * RING, x_to * groups + y_to, flag)
 
     served = None
-    calls = (
-        (("line", 0), ("mid", 0)),
-        (("tail", 0), ("line", 1), ("mid", 1)),
-        (("tail", 1), ("line", 2), ("mid", 2)),
-        (("tail", 2), ("line", 3)),
-        (("tail", 3), ("mid", 3)),
-    )
-    lines_of = {"line": (0,), "mid": (1, 2), "tail": (3,)}
-    parts = {
-        "line": (line, line_before, line_after, line_far),
-        "mid": (mid, mid_before, mid_after, mid_far),
-        "tail": (tail, tail_before, tail_after, tail_far),
-    }
-    for call in calls:
-        places = tuple(RING * piece + j for kind, piece in call for j in lines_of[kind])
-        piece_rows = tuple(parts[kind][piece] for kind, piece in call)
-        served = serve(scalars, places, piece_rows, weights, served, tok_rows, depth)
+    pieces = (
+        (line, mid, tail),
+        (line_before, mid_before, tail_before),
+        (line_after, mid_after, tail_after),
+        (line_far, mid_far, tail_far),
+    )
+    for number, piece in enumerate(pieces):
+        served = serve(scalars, number, piece, weights, served, tok_rows, depth)
 
     lanes = served.shape[2]
     homes = groups * depth

time: 247 us -> 245 us (level)
  Pallas kernels: 39.6 us -> 36.3 us
  waiting for transfers between devices: 85.5 us -> 88.2 us
    ppermute x13, waiting for transfers between devices: 29.3 us -> 36.1 us  [shift(): return lax.ppermute(value, ALL_AXES, pairs)]
    all_to_all x1, starting transfers between devices: 9.54 us -> 13.7 us  [per_device(): lax.all_to_all(send, ('dp', 'z'), split_axis=0, concat_axis=0, tiled=True)]
    ppermute x1, starting transfers between devices: 5.25 us -> 1.92 us  [per_device(): theirs = theirs + (lax.ppermute(mine[1], 'core', swap),)]
    pallas_call x5 -> x4, Pallas kernels: 37.2 us -> 34 us  [serve(): pl.pallas_call(functools.partial(expert_kernel, number=number, tok_rows=t...]
    ppermute x13, starting transfers between devices: 40 us -> 37 us  [shift(): return lax.ppermute(value, ALL_AXES, pairs)]
    all_to_all x1, waiting for transfers between devices: 17.4 us -> 14.5 us  [per_device(): lax.all_to_all(served.reshape(width, homes, lanes), 'x', split_axis=0, co...]
  transfers between devices with their start and end apart: 17 -> 17, of which waited for: 6 -> 6; matrix products, arithmetic and copies ran while one was open for 2% -> 2% of each run, Pallas kernels for 12% -> 11%
where the time goes in v2:
time: 245 us; the launch traced here: 241 us
  waiting for transfers between devices  88.2 us (36%)
  starting transfers between devices  69.7 us (28%)
  Pallas kernels  36.3 us (15%)
  blocking collectives  34.8 us (14%)
  local copies, waits for them, and re-layouts  4.92 us (2%)
  other arithmetic  4.5 us (2%)
    all_to_all x1, waiting for transfers between devices, per_device(): lax.all_to_all(send, ('dp', 'z'), split_axis=0, concat_axis=0, tiled=True)  37.7 us
    ppermute x13, starting transfers between devices, shift(): return lax.ppermute(value, ALL_AXES, pairs)  37 us
    ppermute x13, waiting for transfers between devices, shift(): return lax.ppermute(value, ALL_AXES, pairs)  36.1 us
    all_gather x1, blocking collectives, per_device(): lax.all_gather(jnp.concatenate([tokens, id_part], axis=1), 'z', axis=0, t...  34.8 us
    pallas_call x4, Pallas kernels, serve(): pl.pallas_call(functools.partial(expert_kernel, number=number, tok_rows=t...  34 us
    all_to_all x1, waiting for transfers between devices, per_device(): lax.all_to_all(served.reshape(width, homes, lanes), 'x', split_axis=0, co...  14.5 us
    all_to_all x1, starting transfers between devices, per_device(): lax.all_to_all(send, ('dp', 'z'), split_axis=0, concat_axis=0, tiled=True)  13.7 us
    ppermute x1, starting transfers between devices, per_device(): theirs = (lax.ppermute(mine[0], 'core', swap),)  13.6 us
  transfers between devices with their start and end apart: 17, of which 6 were waited for; matrix products, arithmetic and copies ran while one was open for 2% of the time, Pallas kernels for 11%

profile of v2, /device:TPU:1, one launch (start us, length us, event | category | flops | bytes accessed | tf_op | source)
XLA Modules:
  0.0 240.8 jit_solution(3170365223791713390)
XLA Ops:
  1.5 34.8 %all_gather.3.line_ref = bf16[128,3712]{1,0:T(8,128)(2,1)S(1)} all-gather(bf16[8,3712]{1,0:T(8,128)(2,1)S(1)} %fusion.1), channel_id=1, replica_groups=mesh['dp'=4,'z'=16,'x'=4,'core'=2] {'z'}, dimensions={0}, use_global_device_ids=true | all-gather | bytes 1009664 | tf_op jit(solution)/shard_map/all_gather | solution.py:178
  36.3 3.1 %collective-permute-start.2 = (bf16[128,3712]{1,0:T(8,128)(2,1)S(1)}, bf16[128,3712]{1,0:T(8,128)(2,1)S(1)}, u32[]{:S(2)}, u32[]{:S(2)}) collective-permute-start(bf16[128,3712]{1,0:T(8,128)(2,1)S(1)} %all_gather.3.line_ref), channel_id=1, source_target_pairs={{0,128},{1,3},{2,130},{3,5},{4,132},{5,7},{6,134},{7,1},{8,136},{9... | collective-permute-start | bytes 2850824 | tf_op jit(solution)/shard_map/ppermute | solution.py:173
  39.4 3.4 %collective-permute-start.3 = (bf16[128,3712]{1,0:T(8,128)(2,1)S(1)}, bf16[128,3712]{1,0:T(8,128)(2,1)S(1)}, u32[]{:S(2)}, u32[]{:S(2)}) collective-permute-start(bf16[128,3712]{1,0:T(8,128)(2,1)S(1)} %all_gather.3.line_ref), channel_id=1, source_target_pairs={{0,384},{1,7},{2,386},{3,1},{4,388},{5,3},{6,390},{7,5},{8,392},{9... | collective-permute-start | bytes 2850824 | tf_op jit(solution)/shard_map/ppermute | solution.py:173
  42.8 9.5 %collective-permute-done.2 = bf16[128,3712]{1,0:T(8,128)(2,1)S(1)} collective-permute-done((bf16[128,3712]{1,0:T(8,128)(2,1)S(1)}, bf16[128,3712]{1,0:T(8,128)(2,1)S(1)}, u32[]{:S(2)}, u32[]{:S(2)}) %collective-permute-start.2) | collective-permute-done | bytes 950304 | tf_op jit(solution)/shard_map/ppermute | solution.py:173
  55.2 4.8 %collective-permute-start.4 = (bf16[256,3712]{1,0:T(8,128)(2,1)}, bf16[256,3712]{1,0:T(8,128)(2,1)}, u32[]{:S(2)}, u32[]{:S(2)}) collective-permute-start(bf16[256,3712]{1,0:T(8,128)(2,1)} %constant_dynamic-update-slice_fusion.mid_ref), channel_id=1, source_target_pairs={{0,6},{1,385},{2,0},{3,387},{4,2},{5,389},{6,4},{7,391},{8,14},{9,... | collective-permute-start | bytes 5701640 | tf_op jit(solution)/shard_map/ppermute | solution.py:173
  60.0 3.1 %collective-permute-start.6 = (bf16[64,3712]{1,0:T(8,128)(2,1)S(1)}, bf16[64,3712]{1,0:T(8,128)(2,1)S(1)}, u32[]{:S(2)}, u32[]{:S(2)}) collective-permute-start(bf16[64,3712]{1,0:T(8,128)(2,1)S(1)} %slice.8), channel_id=1, source_target_pairs={{0,128},{1,3},{2,130},{3,5},{4,132},{5,7},{6,134},{7,1},{8,136},{9... | collective-permute-start | bytes 1425416 | tf_op jit(solution)/shard_map/ppermute | solution.py:173
  63.2 3.4 %collective-permute-start.7 = (bf16[64,3712]{1,0:T(8,128)(2,1)S(1)}, bf16[64,3712]{1,0:T(8,128)(2,1)S(1)}, u32[]{:S(2)}, u32[]{:S(2)}) collective-permute-start(bf16[64,3712]{1,0:T(8,128)(2,1)S(1)} %slice.9), channel_id=1, source_target_pairs={{0,384},{1,7},{2,386},{3,1},{4,388},{5,3},{6,390},{7,5},{8,392},{9... | collective-permute-start | bytes 1425416 | tf_op jit(solution)/shard_map/ppermute | solution.py:173
  66.6 13.6 %collective-permute-start.10 = (bf16[3584,256]{1,0:T(8,128)(2,1)S(1)}, bf16[3584,256]{1,0:T(8,128)(2,1)}, u32[]{:S(2)}, u32[]{:S(2)}) collective-permute-start(bf16[3584,256]{1,0:T(8,128)(2,1)S(1)} %bitcast.7), channel_id=1, source_target_pairs={{0,1},{1,0},{2,3},{3,2},{4,5},{5,4},{6,7},{7,6},{8,9},{9,8},{10,11... | collective-permute-start | bytes 5505032 | tf_op jit(solution)/shard_map/ppermute | solution.py:189
  80.2 1.9 collective-permute-start.11
  82.1 2.3 collective-permute-start
  84.4 2.6 %collective-permute-start.14 = (bf16[256,3712]{1,0:T(8,128)(2,1)}, bf16[256,3712]{1,0:T(8,128)(2,1)}, u32[]{:S(2)}, u32[]{:S(2)}) collective-permute-start(bf16[256,3712]{1,0:T(8,128)(2,1)} %constant_dynamic-update-slice_fusion.mid_ref), channel_id=1, source_target_pairs={{0,2},{1,129},{2,4},{3,131},{4,6},{5,133},{6,0},{7,135},{8,10},{9,... | collective-permute-start | bytes 5701640 | tf_op jit(solution)/shard_map/ppermute | solution.py:173
  88.7 9.4 %collective-permute-done.line_ref = bf16[128,3712]{1,0:T(8,128)(2,1)S(1)} collective-permute-done((bf16[128,3712]{1,0:T(8,128)(2,1)S(1)}, bf16[128,3712]{1,0:T(8,128)(2,1)S(1)}, u32[]{:S(2)}, u32[]{:S(2)}) %collective-permute-start) | collective-permute-done | bytes 950304 | tf_op jit(solution)/shard_map/ppermute | solution.py:173
  101.0 4.6 %collective-permute-start.5 = (bf16[256,3712]{1,0:T(8,128)(2,1)}, bf16[256,3712]{1,0:T(8,128)(2,1)}, u32[]{:S(2)}, u32[]{:S(2)}) collective-permute-start(bf16[256,3712]{1,0:T(8,128)(2,1)} %collective-permute-done.4.mid_ref), channel_id=1, source_target_pairs={{0,6},{1,385},{2,0},{3,387},{4,2},{5,389},{6,4},{7,391},{8,14},{9,... | collective-permute-start | bytes 5701640 | tf_op jit(solution)/shard_map/ppermute | solution.py:173
  107.3 1.9 collective-permute-start.12
  112.5 16.3 %collective-permute-done.8.tail_ref = bf16[128,3712]{1,0:T(8,128)(2,1)} collective-permute-done((bf16[128,3712]{1,0:T(8,128)(2,1)}, bf16[128,3712]{1,0:T(8,128)(2,1)}, u32[]{:S(2)}, u32[]{:S(2)}) %collective-permute-start.8) | collective-permute-done | bytes 950304 | tf_op jit(solution)/shard_map/ppermute | solution.py:173
  130.7 2.1 collective-permute-start.9
  132.8 8.6 %expert.4.rest_4_ = bf16[16,16,3072]{2,1,0:T(8,128)(2,1)} custom-call(s32[32]{0:T(128)S(1)} %compare_select_fusion.12.scalar_ref, bf16[128,3712]{1,0:T(8,128)(2,1)S(1)} %all_gather.3.line_ref, bf16[256,3712]{1,0:T(8,128)(2,1)} %constant_dynamic-update-slice_fusion.mid_ref, bf16[128,3712]{1,0:T(8,128)(2,1)} %constant_dynamic-update-slice_fusion.2.tail_ref, ...), custom_call_target="tpu_custom_call" | custom-call | flops 3758096384 | bytes 11534336 | tf_op jit(solution)/shard_map/expert/pallas_call | solution.py:97
  141.4 8.7 %expert.5.rest_4_ = bf16[16,16,3072]{2,1,0:T(8,128)(2,1)} custom-call(s32[32]{0:T(128)S(1)} %compare_select_fusion.12.scalar_ref, bf16[128,3712]{1,0:T(8,128)(2,1)S(1)} %copy-done.2, bf16[256,3712]{1,0:T(8,128)(2,1)} %collective-permute-done.14.mid_ref, bf16[128,3712]{1,0:T(8,128)(2,1)} %collective-permute-done.8.tail_ref, ...), custom_call_target="tpu_custom_call", output_to_operand_aliasing={{}: (8, {})} | custom-call | flops 3758096384 | bytes 11534336 | tf_op jit(solution)/shard_map/expert/pallas_call | solution.py:97
  150.1 8.3 %expert.6.rest_4_ = bf16[16,16,3072]{2,1,0:T(8,128)(2,1)} custom-call(s32[32]{0:T(128)S(1)} %compare_select_fusion.12.scalar_ref, bf16[128,3712]{1,0:T(8,128)(2,1)S(1)} %collective-permute-done.12.line_ref, bf16[256,3712]{1,0:T(8,128)(2,1)} %collective-permute-done.4.mid_ref, ...), custom_call_target="tpu_custom_call", output_to_operand_aliasing={{}: (8, {})} | custom-call | flops 3758096384 | bytes 11534336 | tf_op jit(solution)/shard_map/expert/pallas_call | solution.py:97
  158.5 8.4 %expert.7 = bf16[16,16,3072]{2,1,0:T(8,128)(2,1)} custom-call(s32[32]{0:T(128)S(1)} %compare_select_fusion.12.scalar_ref, bf16[128,3712]{1,0:T(8,128)(2,1)S(1)} %collective-permute-done.1.line_ref, bf16[256,3712]{1,0:T(8,128)(2,1)} %collective-permute-done.5.mid_ref, ...), custom_call_target="tpu_custom_call", output_to_operand_aliasing={{}: (8, {})} | custom-call | flops 3758096384 | bytes 11534336 | tf_op jit(solution)/shard_map/expert/pallas_call | solution.py:97
  166.8 3.6 %all-to-all-start = ((bf16[4,64,3072]{2,1,0:T(8,128)(2,1)}), bf16[4,64,3072]{2,1,0:T(8,128)(2,1)S(1)}, u32[]{:S(2)}, u32[]{:S(2)}) async-start(bf16[4,64,3072]{2,1,0:T(8,128)(2,1)} %bitcast.3), calls=%async_computation | async-start | bytes 3145728 | tf_op jit(solution)/shard_map/all_to_all | solution.py:241
  172.4 14.5 %all-to-all-done.near_ref = bf16[4,64,3072]{2,1,0:T(8,128)(2,1)S(1)} async-done(((bf16[4,64,3072]{2,1,0:T(8,128)(2,1)}), bf16[4,64,3072]{2,1,0:T(8,128)(2,1)S(1)}, u32[]{:S(2)}, u32[]{:S(2)}) %all-to-all-start) | async-done | bytes 1572896 | tf_op jit(solution)/shard_map/all_to_all | solution.py:241
  188.3 13.7 %all-to-all-start.1 = ((bf16[64,24,256]{2,1,0:T(8,128)(2,1)}), bf16[64,24,256]{2,1,0:T(8,128)(2,1)S(1)}, u32[]{:S(2)}, u32[]{:S(2)}) async-start(bf16[64,24,256]{2,1,0:T(8,128)(2,1)} %bitcast.4), calls=%async_computation.1 | async-start | bytes 1572864 | tf_op jit(solution)/shard_map/all_to_all | solution.py:255
  202.2 37.7 %all-to-all-done.1 = bf16[64,24,256]{2,1,0:T(8,128)(2,1)S(1)} async-done(((bf16[64,24,256]{2,1,0:T(8,128)(2,1)}), bf16[64,24,256]{2,1,0:T(8,128)(2,1)S(1)}, u32[]{:S(2)}, u32[]{:S(2)}) %all-to-all-start.1) | async-done | bytes 786464 | tf_op jit(solution)/shard_map/all_to_all | solution.py:255
  (44 shorter events, 18.4 us)
Async XLA Ops:
  36.3 16.0 %collective-permute-start.2 = (bf16[128,3712]{1,0:T(8,128)(2,1)S(1)}, bf16[128,3712]{1,0:T(8,128)(2,1)S(1)}, u32[]{:S(2)}, u32[]{:S(2)}) collective-permute-start(bf16[128,3712]{1,0:T(8,128)(2,1)S(1)} %all_gather.3.line_ref), channel_id=1, source_target_pairs={{0,128},{1,3},{2,130},{3,5},{4,132},{5,7},{6,134},{7,1},{8,136},{9... | collective-permute-start | bytes 2850824 | tf_op jit(solution)/shard_map/ppermute | solution.py:173
  39.4 14.8 %collective-permute-start.3 = (bf16[128,3712]{1,0:T(8,128)(2,1)S(1)}, bf16[128,3712]{1,0:T(8,128)(2,1)S(1)}, u32[]{:S(2)}, u32[]{:S(2)}) collective-permute-start(bf16[128,3712]{1,0:T(8,128)(2,1)S(1)} %all_gather.3.line_ref), channel_id=1, source_target_pairs={{0,384},{1,7},{2,386},{3,1},{4,388},{5,3},{6,390},{7,5},{8,392},{9... | collective-permute-start | bytes 2850824 | tf_op jit(solution)/shard_map/ppermute | solution.py:173
  53.3 13.2 %copy-start = (bf16[1,3584,256]{2,1,0:T(8,128)(2,1)S(1)}, bf16[1,3584,256]{2,1,0:T(8,128)(2,1)}, u32[]{:S(2)}) copy-start(bf16[1,3584,256]{2,1,0:T(8,128)(2,1)} %param.8) | copy-start | bytes 5505028
  55.2 50.5 %copy-start.3 = (s32[8,8]{1,0:T(8,128)S(1)}, s32[8,8]{1,0:T(8,128)}, u32[]{:S(2)}) copy-start(s32[8,8]{1,0:T(8,128)} %param.6) | copy-start | bytes 772
  55.2 45.9 %collective-permute-start.4 = (bf16[256,3712]{1,0:T(8,128)(2,1)}, bf16[256,3712]{1,0:T(8,128)(2,1)}, u32[]{:S(2)}, u32[]{:S(2)}) collective-permute-start(bf16[256,3712]{1,0:T(8,128)(2,1)} %constant_dynamic-update-slice_fusion.mid_ref), channel_id=1, source_target_pairs={{0,6},{1,385},{2,0},{3,387},{4,2},{5,389},{6,4},{7,391},{8,14},{9,... | collective-permute-start | bytes 5701640 | tf_op jit(solution)/shard_map/ppermute | solution.py:173
  60.0 22.1 %collective-permute-start.6 = (bf16[64,3712]{1,0:T(8,128)(2,1)S(1)}, bf16[64,3712]{1,0:T(8,128)(2,1)S(1)}, u32[]{:S(2)}, u32[]{:S(2)}) collective-permute-start(bf16[64,3712]{1,0:T(8,128)(2,1)S(1)} %slice.8), channel_id=1, source_target_pairs={{0,128},{1,3},{2,130},{3,5},{4,132},{5,7},{6,134},{7,1},{8,136},{9... | collective-permute-start | bytes 1425416 | tf_op jit(solution)/shard_map/ppermute | solution.py:173
  63.2 21.2 %collective-permute-start.7 = (bf16[64,3712]{1,0:T(8,128)(2,1)S(1)}, bf16[64,3712]{1,0:T(8,128)(2,1)S(1)}, u32[]{:S(2)}, u32[]{:S(2)}) collective-permute-start(bf16[64,3712]{1,0:T(8,128)(2,1)S(1)} %slice.9), channel_id=1, source_target_pairs={{0,384},{1,7},{2,386},{3,1},{4,388},{5,3},{6,390},{7,5},{8,392},{9... | collective-permute-start | bytes 1425416 | tf_op jit(solution)/shard_map/ppermute | solution.py:173
  66.6 40.7 %collective-permute-start.10 = (bf16[3584,256]{1,0:T(8,128)(2,1)S(1)}, bf16[3584,256]{1,0:T(8,128)(2,1)}, u32[]{:S(2)}, u32[]{:S(2)}) collective-permute-start(bf16[3584,256]{1,0:T(8,128)(2,1)S(1)} %bitcast.7), channel_id=1, source_target_pairs={{0,1},{1,0},{2,3},{3,2},{4,5},{5,4},{6,7},{7,6},{8,9},{9,8},{10,11... | collective-permute-start | bytes 5505032 | tf_op jit(solution)/shard_map/ppermute | solution.py:189
  80.2 29.1 %collective-permute-start.11 = (bf16[3584,256]{1,0:T(8,128)(2,1)}, bf16[3584,256]{1,0:T(8,128)(2,1)}, u32[]{:S(2)}, u32[]{:S(2)}) collective-permute-start(bf16[3584,256]{1,0:T(8,128)(2,1)} %bitcast.2.rest_1_), channel_id=1, source_target_pairs={{0,1},{1,0},{2,3},{3,2},{4,5},{5,4},{6,7},{7,6},{8,9},{9,8},{10,11... | collective-permute-start | bytes 5505032 | tf_op jit(solution)/shard_map/ppermute | solution.py:190
  82.1 16.0 %collective-permute-start = (bf16[128,3712]{1,0:T(8,128)(2,1)S(1)}, bf16[128,3712]{1,0:T(8,128)(2,1)S(1)}, u32[]{:S(2)}, u32[]{:S(2)}) collective-permute-start(bf16[128,3712]{1,0:T(8,128)(2,1)S(1)} %all_gather.3.line_ref), channel_id=1, source_target_pairs={{0,2},{1,129},{2,4},{3,131},{4,6},{5,133},{6,0},{7,135},{8,10},{9,... | collective-permute-start | bytes 2850824 | tf_op jit(solution)/shard_map/ppermute | solution.py:173
  84.4 46.3 %collective-permute-start.14 = (bf16[256,3712]{1,0:T(8,128)(2,1)}, bf16[256,3712]{1,0:T(8,128)(2,1)}, u32[]{:S(2)}, u32[]{:S(2)}) collective-permute-start(bf16[256,3712]{1,0:T(8,128)(2,1)} %constant_dynamic-update-slice_fusion.mid_ref), channel_id=1, source_target_pairs={{0,2},{1,129},{2,4},{3,131},{4,6},{5,133},{6,0},{7,135},{8,10},{9,... | collective-permute-start | bytes 5701640 | tf_op jit(solution)/shard_map/ppermute | solution.py:173
  98.1 1.0 copy-start.1
  99.1 29.6 %collective-permute-start.8 = (bf16[128,3712]{1,0:T(8,128)(2,1)}, bf16[128,3712]{1,0:T(8,128)(2,1)}, u32[]{:S(2)}, u32[]{:S(2)}) collective-permute-start(bf16[128,3712]{1,0:T(8,128)(2,1)} %constant_dynamic-update-slice_fusion.2.tail_ref), channel_id=1, source_target_pairs={{0,2},{1,129},{2,4},{3,131},{4,6},{5,133},{6,0},{7,135},{8,10},{9,... | collective-permute-start | bytes 2850824 | tf_op jit(solution)/shard_map/ppermute | solution.py:173
  101.0 57.4 %collective-permute-start.5 = (bf16[256,3712]{1,0:T(8,128)(2,1)}, bf16[256,3712]{1,0:T(8,128)(2,1)}, u32[]{:S(2)}, u32[]{:S(2)}) collective-permute-start(bf16[256,3712]{1,0:T(8,128)(2,1)} %collective-permute-done.4.mid_ref), channel_id=1, source_target_pairs={{0,6},{1,385},{2,0},{3,387},{4,2},{5,389},{6,4},{7,391},{8,14},{9,... | collective-permute-start | bytes 5701640 | tf_op jit(solution)/shard_map/ppermute | solution.py:173
  107.3 42.8 %collective-permute-start.12 = (bf16[128,3712]{1,0:T(8,128)(2,1)S(1)}, bf16[128,3712]{1,0:T(8,128)(2,1)S(1)}, u32[]{:S(2)}, u32[]{:S(2)}) collective-permute-start(bf16[128,3712]{1,0:T(8,128)(2,1)S(1)} %all_gather.3.line_ref), channel_id=1, source_target_pairs={{0,6},{1,385},{2,0},{3,387},{4,2},{5,389},{6,4},{7,391},{8,14},{9,... | collective-permute-start | bytes 2850824 | tf_op jit(solution)/shard_map/ppermute | solution.py:173
  109.2 40.9 %collective-permute-start.13 = (bf16[128,3712]{1,0:T(8,128)(2,1)}, bf16[128,3712]{1,0:T(8,128)(2,1)S(1)}, u32[]{:S(2)}, u32[]{:S(2)}) collective-permute-start(bf16[128,3712]{1,0:T(8,128)(2,1)} %constant_dynamic-update-slice_fusion.2.tail_ref), channel_id=1, source_target_pairs={{0,6},{1,385},{2,0},{3,387},{4,2},{5,389},{6,4},{7,391},{8,14},{9,... | collective-permute-start | bytes 2850824 | tf_op jit(solution)/shard_map/ppermute | solution.py:173
  112.5 29.0 %copy-start.2 = (bf16[128,3712]{1,0:T(8,128)(2,1)S(1)}, bf16[128,3712]{1,0:T(8,128)(2,1)}, u32[]{:S(2)}) copy-start(bf16[128,3712]{1,0:T(8,128)(2,1)} %copy-done.1) | copy-start | bytes 2850820
  128.8 29.7 %collective-permute-start.1 = (bf16[128,3712]{1,0:T(8,128)(2,1)}, bf16[128,3712]{1,0:T(8,128)(2,1)S(1)}, u32[]{:S(2)}, u32[]{:S(2)}) collective-permute-start(bf16[128,3712]{1,0:T(8,128)(2,1)} %copy-done.1), channel_id=1, source_target_pairs={{0,2},{1,129},{2,4},{3,131},{4,6},{5,133},{6,0},{7,135},{8,10},{9,... | collective-permute-start | bytes 2850824 | tf_op jit(solution)/shard_map/ppermute | solution.py:173
  130.7 27.8 %collective-permute-start.9 = (bf16[128,3712]{1,0:T(8,128)(2,1)}, bf16[128,3712]{1,0:T(8,128)(2,1)S(1)}, u32[]{:S(2)}, u32[]{:S(2)}) collective-permute-start(bf16[128,3712]{1,0:T(8,128)(2,1)} %collective-permute-done.8.tail_ref), channel_id=1, source_target_pairs={{0,2},{1,129},{2,4},{3,131},{4,6},{5,133},{6,0},{7,135},{8,10},{9,... | collective-permute-start | bytes 2850824 | tf_op jit(solution)/shard_map/ppermute | solution.py:173
  166.8 20.0 %all-to-all-start = ((bf16[4,64,3072]{2,1,0:T(8,128)(2,1)}), bf16[4,64,3072]{2,1,0:T(8,128)(2,1)S(1)}, u32[]{:S(2)}, u32[]{:S(2)}) async-start(bf16[4,64,3072]{2,1,0:T(8,128)(2,1)} %bitcast.3), calls=%async_computation | async-start | bytes 3145728 | tf_op jit(solution)/shard_map/all_to_all | solution.py:241
  186.9 15.2 %copy-start.4 = (f32[8,8]{1,0:T(8,128)S(1)}, f32[8,8]{1,0:T(8,128)}, u32[]{:S(2)}) copy-start(f32[8,8]{1,0:T(8,128)} %param.7) | copy-start | bytes 772
  188.3 51.6 %all-to-all-start.1 = ((bf16[64,24,256]{2,1,0:T(8,128)(2,1)}), bf16[64,24,256]{2,1,0:T(8,128)(2,1)S(1)}, u32[]{:S(2)}, u32[]{:S(2)}) async-start(bf16[64,24,256]{2,1,0:T(8,128)(2,1)} %bitcast.4), calls=%async_computation.1 | async-start | bytes 1572864 | tf_op jit(solution)/shard_map/all_to_all | solution.py:255
